TPU v7x, 256 devices: a whole 4x4x8 slice. The times are simulated.
256 devices in a mesh: gx: 16 (over z, core), gy: 4 (over x), ens: 4 (over y).
Axes of the slice: x: 4, y: 4, z: 8, core: 2. Of those that a mesh axis runs over, the one named last changes fastest.
Arguments:
- state: float32 [16, 80, 128, 512], P(None, 'ens', 'gx', 'gy'), may hold values from -6 to 6
- obs_value: float32 [4, 256], replicated, may hold values from -6 to 6
- obs_error: float32 [4, 256], replicated, may hold values from 0.25 to 2
- obs_where: int32 [4, 3, 256], replicated, may hold values from 0 to 511, as said below
- radius: int32 [4, 256], replicated, may hold values from 33 to 43
- wind: float32 [2, 16, 128, 512], P(None, None, 'gx', 'gy'), may hold values from -0.4 to 0.4
Outputs:
- forecast: float32 [16, 80, 128, 512], P(None, 'ens', 'gx', 'gy')
Inputs may be any that keep to these rules, and one draw needn't show every extreme that they name: obs_where[b, 0] is a level below 16, obs_where[b, 1] a row below 128, obs_where[b, 2] a column below 512.
All inputs are finite; a program needn't handle non-finite values.
Results may differ from a plain program's by a relative error of at most 0.00012.
Values sent between devices are 32-bit elements; how exact they have to be, the bound alone decides.
No kernel may reach another device: no remote copies, remote signals or barrier semaphores. Data moves between devices by JAX's collectives and lax.ppermute only.
A program may use at most 64 MiB of HBM per device.

v0:
```python
import jax
import jax.numpy as jnp
from jax import lax
from jax.experimental import pallas as pl
from jax.experimental.pallas import tpu as pltpu
from jax.sharding import Mesh
from jax.sharding import PartitionSpec as P


GX = ("gx_0", "gx_1")
EPSILON = 1e-06
DIFFUSE = 0.05
F32 = jnp.float32
BF16 = jnp.bfloat16
ROWS = 2
VMEM = pltpu.VMEM
SMEM = pltpu.SMEM


def split(x):
    high = x.astype(BF16)
    return high, (x - high.astype(F32)).astype(BF16)


def pick_kernel(place_ref, where_ref, state_ref, keep_ref, give_ref, parts_ref, found_ref):
    row_start, col_start, core = place_ref[0], place_ref[1], place_ref[2]
    cells = state_ref.shape[0] // 8
    levels = found_ref.shape[0] // keep_ref.shape[0]
    members = keep_ref.shape[0]
    cols = state_ref.shape[1]
    n_obs = where_ref.shape[2]
    halves = where_ref.shape[0] // 2
    for row in range(8):
        x = state_ref[pl.ds(row, cells, stride=8), :]
        high = x.astype(BF16)
        rest = x - high.astype(F32)
        mid = rest.astype(BF16)
        low = (rest - mid.astype(F32)).astype(BF16)
        for at, part in enumerate((high, mid, low)):
            parts_ref[at * cells : (at + 1) * cells, row * cols : (row + 1) * cols] = part
    cell = lax.broadcasted_iota(jnp.int32, (8 * cols, n_obs), 0)
    for half, out_ref in enumerate((keep_ref, give_ref)):
        for at in range(halves):
            batch = lax.rem(core + half, 2) * halves + at
            places = where_ref[batch]
            lev = places[0:1, :]
            row = places[1:2, :] - row_start
            col = places[2:3, :] - col_start
            owned = (row >= 0) & (row < 8) & (col >= 0) & (col < cols)
            key = jnp.where(owned, row * cols + col, -1)
            hot = jnp.where(cell == key, 1.0, 0.0).astype(BF16)
            got = jnp.dot(parts_ref[...], hot, preferred_element_type=F32)
            found_ref[...] = got[:cells] + got[cells : 2 * cells] + got[2 * cells :]
            total = jnp.zeros((members, n_obs), F32)
            for level in range(levels):
                rows = found_ref[level * members : (level + 1) * members, :]
                total = total + jnp.where(lev == level, rows, 0.0)
            out_ref[:, at * n_obs : (at + 1) * n_obs] = total


def taper(dist_sq, reach):
    weight = jnp.maximum(0.0, 1.0 - dist_sq * reach)
    return weight * weight


def down(row):
    return jnp.transpose(jnp.broadcast_to(row, (128, row.shape[1])))


def wide(block, lanes):
    return jnp.concatenate([block] * (lanes // 128), axis=1)


def lay_kernel(place_ref, cur_ref, after_ref, y_ref, top_ref, low_ref, left_ref, right_ref):
    me = place_ref[3]
    cols = cur_ref.shape[1]
    shares = 4
    levels = y_ref.shape[2] // cols
    members = y_ref.shape[1] // shares
    for share in range(shares):
        source = lax.rem(me + share, shares)
        for level in range(levels):
            base = (source * levels + level) * members * 8
            for row in range(8):
                got = cur_ref[pl.ds(base + row, members, stride=8), :]
                y_ref[row, share * members : (share + 1) * members, level * cols : (level + 1) * cols] = got
    top_ref[...] = y_ref[0]
    low_ref[...] = y_ref[7]
    lane = lax.broadcasted_iota(jnp.int32, left_ref.shape, 1)
    left = jnp.zeros(left_ref.shape, F32)
    right = jnp.zeros(left_ref.shape, F32)
    for level in range(levels):
        for row in range(8):
            x = y_ref[row, :, level * cols : (level + 1) * cols]
            at = level * 8 + row
            left = jnp.where(lane == 32 + at, pltpu.roll(x, 32 + at, 1), left)
            right = jnp.where(lane == at, pltpu.roll(x, (at + 1) % cols, 1), right)
    left_ref[...] = left
    right_ref[...] = right


def taper_kernel(place_ref, where_ref, radius_ref, after_ref, w_ref, wc_ref, wo_ref):
    row_start, col_start = place_ref[0], place_ref[1]
    batches, _, n_obs = where_ref.shape
    cols = w_ref.shape[2]
    lane_w = lax.broadcasted_iota(jnp.int32, (n_obs, cols), 1)
    for batch in range(batches):
        places = where_ref[batch].astype(F32)
        q = radius_ref[batch : batch + 1, :].astype(F32)
        obs_row, obs_col = down(places[1:2, :]), down(places[2:3, :])
        reach = down(1.0 / (4.0 * q * q))
        gap = (lane_w + col_start).astype(F32) - obs_col
        gap = gap * gap
        for row in range(10):
            off = (row_start + (row - 1)).astype(F32) - obs_row
            w_ref[batch * 10 + row] = taper(off * off + gap, reach)
        edge_row = (row_start + lane_w % 8).astype(F32) - obs_row
        edge_col = jnp.where(lane_w < 32, col_start - 1, col_start + cols).astype(F32) - obs_col
        wc_ref[batch] = taper(edge_row * edge_row + edge_col * edge_col, reach)
        for later in range(batch + 1, batches):
            others = where_ref[later].astype(F32)
            off = others[1:2, :] - wide(obs_row, n_obs)
            gap_o = others[2:3, :] - wide(obs_col, n_obs)
            pair = batch * (2 * batches - batch - 1) // 2 + later - batch - 1
            wo_ref[pair] = taper(off * off + gap_o * gap_o, wide(reach, n_obs))


def changed(xs, weights, s3, n2):
    members = xs[0].shape[0]
    stacks = []
    for x in xs:
        mean = jnp.sum(x, axis=0, keepdims=True) * (1.0 / members)
        a_high, a_low = split(x - mean)
        stacks.append(jnp.concatenate([a_high, a_high, a_low], axis=0))
    covars = [jnp.dot(s3, a3, preferred_element_type=F32) for a3 in stacks]
    gains = [split(w * c) for w, c in zip(weights, covars)]
    outs = []
    for x, (g_high, g_low) in zip(xs, gains):
        both = jnp.dot(n2, g_high, preferred_element_type=F32)
        rest = jnp.dot(n2[:members], g_low, preferred_element_type=F32)
        outs.append(x + ((both[:members] + both[members:]) + rest))
    return outs


def main_kernel(
    place_ref, value_ref, error_ref, own_ref, one_ref, two_ref, three_ref, other_ref,
    y_ref, up_ref, down_ref, left_ref, right_ref, w_ref, wc_ref, wo_ref, wind_ref,
    out_ref, prior_ref, z_ref, edge_ref, s3_ref, n2_ref, f_ref,
):
    core, me, lev_start = place_ref[2], place_ref[3], place_ref[4]
    batches, n_obs = value_ref.shape
    members = z_ref.shape[1]
    shares = 4
    share_size = members // shares
    cols = w_ref.shape[2]
    levels = z_ref.shape[2] // cols
    half = own_ref.shape[1]
    for share, ref in enumerate((own_ref, one_ref, two_ref, three_ref)):
        rows = slice(share * share_size, (share + 1) * share_size)
        prior_ref[core, rows, :] = ref[...]
        prior_ref[1 - core, rows, :] = other_ref[share]
    z_ref[0] = up_ref[...]
    z_ref[9] = down_ref[...]
    for row in range(8):
        z_ref[row + 1] = y_ref[row]
    edge_ref[...] = left_ref[...] + right_ref[...]
    per_half = half // n_obs

    def lanes(batch):
        at = batch % per_half
        return batch // per_half, slice(at * n_obs, (at + 1) * n_obs)

    for batch in range(batches):
        part, here = lanes(batch)
        priors = prior_ref[part, :, here]
        value, error = value_ref[batch : batch + 1, :], error_ref[batch : batch + 1, :]
        center = jnp.sum(priors, axis=0, keepdims=True) * (1.0 / members)
        spread = priors - center
        variance = jnp.sum(spread * spread, axis=0, keepdims=True) / (members - 1)
        summed = variance + error
        post_mean = (error * center + variance * value) / summed
        factor = jnp.sqrt(error / summed)
        nudges = post_mean + factor * spread - priors
        inverse = 1.0 / ((members - 1) * (variance + EPSILON))
        n_high, n_low = split(nudges * inverse)
        n2_ref[...] = jnp.concatenate([n_high, n_low], axis=0)
        s_high, s_low = split(spread)
        s3 = jnp.concatenate([s_high.astype(F32), s_low.astype(F32), s_high.astype(F32)], axis=0)
        s3_ref[...] = jnp.transpose(s3).astype(BF16)
        laters = range(batch + 1, batches)
        first = batch * (2 * batches - batch - 1) // 2
        blocks = [edge_ref[...]] + [prior_ref[lanes(k)[0], :, lanes(k)[1]] for k in laters]
        tapers = [wc_ref[batch]] + [wo_ref[first + k] for k in range(len(laters))]
        blocks = changed(blocks, tapers, s3_ref[...], n2_ref[...])
        edge_ref[...] = blocks[0]
        for k, block in zip(laters, blocks[1:]):
            prior_ref[lanes(k)[0], :, lanes(k)[1]] = block

        def step(at, carry):
            rows = [ROWS * at + k for k in range(ROWS)]
            xs = [z_ref[row, :, k * 256 : (k + 1) * 256] for row in rows for k in range(2)]
            ws = [wide(w_ref[batch * 10 + row], 256) for row in rows for _ in range(2)]
            outs = changed(xs, ws, s3_ref[...], n2_ref[...])
            for at_out, out in enumerate(outs):
                k = at_out % 2
                z_ref[rows[at_out // 2], :, k * 256 : (k + 1) * 256] = out
            return carry

        lax.fori_loop(0, 10 // ROWS, step, 0)

    lane = lax.broadcasted_iota(jnp.int32, (members, cols), 1)

    def transport(row, carry):
        edge = edge_ref[...]
        for level in range(levels):
            span = slice(level * cols, (level + 1) * cols)
            a = wind_ref[0, lev_start + level, pl.ds(row, 1), :]
            b = wind_ref[1, lev_start + level, pl.ds(row, 1), :]
            to_up = jnp.maximum(a, 0.0) + DIFFUSE
            to_down = DIFFUSE - jnp.minimum(a, 0.0)
            to_left = jnp.maximum(b, 0.0) + DIFFUSE
            to_right = DIFFUSE - jnp.minimum(b, 0.0)
            stay = 1.0 - ((to_up + to_down) + (to_left + to_right))
            x = z_ref[row + 1, :, span]
            at = level * 8 + row
            left = jnp.where(lane == 0, pltpu.roll(edge, lax.rem(cols - at, cols), 1), pltpu.roll(x, 1, 1))
            right = jnp.where(
                lane == cols - 1, pltpu.roll(edge, cols - 33 - at, 1), pltpu.roll(x, cols - 1, 1)
            )
            f_ref[...] = (
                stay * x + to_up * z_ref[row, :, span] + to_down * z_ref[row + 2, :, span]
                + to_left * left + to_right * right
            )
            for share in range(shares):
                target = lax.rem(me + share, shares)
                base = (target * levels + level) * share_size * 8
                out_ref[pl.ds(base + row, share_size, stride=8), :] = f_ref[
                    share * share_size : (share + 1) * share_size, :
                ]
        return carry

    lax.fori_loop(0, 8, transport, 0)


def ring(axis, shift):
    n = lax.axis_size(axis)
    return [(i, (i + shift) % n) for i in range(n)]


def line(axis, shift):
    n = lax.axis_size(axis)
    return [(i, i + shift) for i in range(n) if 0 <= i + shift < n]


def exchanges():
    cores = lax.axis_size("gx_1")
    depth, across = lax.axis_size("gx_0"), lax.axis_size("gy")
    far = [1 << k for k in range(depth.bit_length() - 1)]
    near = [1 << k for k in range(across.bit_length() - 1)]
    orders = (
        [("x", b) for b in near] + [("z", b) for b in far],
        [("z", b) for b in reversed(far)] + [("x", b) for b in near],
    )
    steps = []
    for at in range(len(orders[0])):
        pairs = []
        for z in range(depth):
            for core in range(cores):
                for x in range(across):
                    axis, bit = orders[core % 2][at]
                    to_z, to_x = (z ^ bit, x) if axis == "z" else (z, x ^ bit)
                    pairs.append(((z * cores + core) * across + x, (to_z * cores + core) * across + to_x))
        steps.append(pairs)
    return steps


def shards(state, obs_value, obs_error, obs_where, radius, wind):
    levels, share_size, tile_rows, tile_cols = state.shape
    shares = lax.axis_size("ens")
    members = share_size * shares
    here = levels // shares
    batches, n_obs = obs_value.shape
    half = batches // 2 * n_obs
    me = lax.axis_index("ens")
    place = jnp.stack(
        [lax.axis_index(GX) * tile_rows, lax.axis_index("gy") * tile_cols, lax.axis_index("gx_1"), me, me * here]
    ).astype(jnp.int32)
    flat = levels * share_size * tile_rows
    vmem = pl.BlockSpec(memory_space=VMEM)
    smem = pl.BlockSpec(memory_space=SMEM)
    cells = levels * share_size
    keep, give = pl.pallas_call(
        pick_kernel,
        out_shape=[jax.ShapeDtypeStruct((share_size, half), F32)] * 2,
        in_specs=[smem, vmem, vmem],
        out_specs=[vmem, vmem],
        scratch_shapes=[VMEM((3 * cells, tile_rows * tile_cols), BF16), VMEM((cells, n_obs), F32)],
        compiler_params=pltpu.CompilerParams(vmem_limit_bytes=16 << 20),
        name="pick",
    )(place, obs_where, state.reshape(flat, tile_cols))
    any_ = pl.BlockSpec(memory_space=pl.ANY)
    cur = lax.all_to_all(state, "ens", split_axis=0, concat_axis=0, tiled=True)
    x = keep + lax.ppermute(give, "gx_1", ring("gx_1", 1))
    for step, pairs in enumerate(exchanges(), start=1):
        got = lax.ppermute(x, (*GX, "gy"), pairs)
        if step == 3:
            line_shape = jax.ShapeDtypeStruct((members, here * tile_cols), F32)
            edge_shape = jax.ShapeDtypeStruct((members, tile_cols), F32)
            y, top, low, left, right = pl.pallas_call(
                lay_kernel,
                out_shape=[
                    jax.ShapeDtypeStruct((tile_rows, members, here * tile_cols), F32),
                    line_shape, line_shape, edge_shape, edge_shape,
                ],
                in_specs=[smem, vmem, any_],
                out_specs=[vmem] * 5,
                compiler_params=pltpu.CompilerParams(vmem_limit_bytes=12 << 20),
                cost_estimate=pl.CostEstimate(flops=2_000_000, bytes_accessed=4_000_000, transcendentals=0),
                name="lay",
            )(place, cur.reshape(flat, tile_cols), x)
            up = lax.ppermute(low, GX, line(GX, 1))
            down_ = lax.ppermute(top, GX, line(GX, -1))
            from_left = lax.ppermute(right, "gy", line("gy", 1))
            from_right = lax.ppermute(left, "gy", line("gy", -1))
            got, y = lax.optimization_barrier((got, y))
        x = x + got
    own = x
    gathered = [own]
    for k in (1, 2, 3):
        gathered.append(lax.ppermute(own, "ens", ring("ens", -k)))
    own, one, two, three, up, down_, from_left, from_right = lax.optimization_barrier(
        (*gathered, up, down_, from_left, from_right)
    )
    stacked = jnp.stack([own, one, two, three])
    other = lax.ppermute(stacked, "gx_1", ring("gx_1", 1))
    pairs = batches * (batches - 1) // 2
    w, wc, wo = pl.pallas_call(
        taper_kernel,
        out_shape=[
            jax.ShapeDtypeStruct((batches * 10, n_obs, tile_cols), F32),
            jax.ShapeDtypeStruct((batches, n_obs, tile_cols), F32),
            jax.ShapeDtypeStruct((pairs, n_obs, n_obs), F32),
        ],
        in_specs=[smem, vmem, vmem, any_],
        out_specs=[vmem] * 3,
        compiler_params=pltpu.CompilerParams(vmem_limit_bytes=20 << 20),
        cost_estimate=pl.CostEstimate(flops=20_000_000, bytes_accessed=8_000_000, transcendentals=0),
        name="taper",
    )(place, obs_where, radius, stacked)
    out = pl.pallas_call(
        main_kernel,
        out_shape=jax.ShapeDtypeStruct((flat, tile_cols), F32),
        in_specs=[smem] + [vmem] * 16,
        out_specs=vmem,
        scratch_shapes=[
            VMEM((2, members, half), F32),
            VMEM((tile_rows + 2, members, here * tile_cols), F32),
            VMEM((members, tile_cols), F32),
            VMEM((n_obs, 3 * members), BF16),
            VMEM((2 * members, n_obs), BF16),
            VMEM((members, tile_cols), F32),
        ],
        compiler_params=pltpu.CompilerParams(vmem_limit_bytes=32 << 20),
        name="main",
    )(
        place, obs_value, obs_error, own, one, two, three, other,
        y, up, down_, from_left, from_right, w, wc, wo, wind,
    )
    out = out.reshape(levels, share_size, tile_rows, tile_cols)
    return lax.all_to_all(out, "ens", split_axis=0, concat_axis=0, tiled=True)


def solution(mesh):
    torus = Mesh(
        mesh.devices.reshape(8, 2, mesh.shape["gy"], mesh.shape["ens"]),
        ("gx_0", "gx_1", "gy", "ens"),
    )
    placed = (P(None, "ens", GX, "gy"), P(), P(), P(), P(), P(None, None, GX, "gy"))

    return jax.shard_map(
        shards, mesh=torus, in_specs=placed, out_specs=P(None, "ens", GX, "gy"), check_vma=False
    )
```

profile of v0, /device:TPU:1, one launch (start us, length us, event | category | flops | bytes accessed | tf_op | source)
XLA Modules:
  0.0 98.8 jit_solution(8989729492159228726)
XLA Ops:
  0.0 0.0 copy-start
  0.0 0.0 copy-start.5
  0.0 5.1 %all-to-all-start = ((f32[16,20,8,128]{3,2,1,0:T(8,128)}), f32[16,20,8,128]{3,2,1,0:T(8,128)S(1)}, u32[]{:S(2)}, u32[]{:S(2)}) async-start(f32[16,20,8,128]{3,2,1,0:T(8,128)} %param.6), calls=%async_computation | async-start | bytes 2621440 | tf_op jit(solution)/shard_map/all_to_all | solution.py:302
  5.1 0.0 copy-done.5
  5.2 0.1 stack.38.place_ref
  5.3 0.0 copy-done
  5.3 2.8 %pick.1 = (f32[20,512]{1,0:T(8,128)S(1)}, f32[20,512]{1,0:T(8,128)S(1)}) custom-call(s32[5]{0:T(128)S(1)} %stack.38.place_ref, s32[4,3,256]{2,1,0:T(4,128)S(1)} %copy.7.where_ref, f32[2560,128]{1,0:T(8,128)S(1)} %bitcast.13), custom_call_target="tpu_custom_call" | custom-call | tf_op jit(solution)/shard_map/pick/pallas_call | solution.py:292
  8.1 1.9 %collective-permute-start = (f32[20,512]{1,0:T(8,128)S(1)}, f32[20,512]{1,0:T(8,128)S(1)}, u32[]{:S(2)}, u32[]{:S(2)}) collective-permute-start(f32[20,512]{1,0:T(8,128)S(1)} %get-tuple-element.26), channel_id=1, source_target_pairs={{0,16},{16,0},{1,17},{17,1},{2,18},{18,2},{3,19},{19,3},{4,20},{20... | collective-permute-start | bytes 122888 | tf_op jit(solution)/shard_map/ppermute | solution.py:303
  10.0 0.9 collective-permute-done
  10.9 6.2 %collective-permute-start.1 = (f32[20,512]{1,0:T(8,128)S(1)}, f32[20,512]{1,0:T(8,128)S(1)}, u32[]{:S(2)}, u32[]{:S(2)}) collective-permute-start(f32[20,512]{1,0:T(8,128)S(1)} %add.22), channel_id=1, source_target_pairs={{0,4},{4,0},{8,12},{12,8},{16,144},{20,148},{24,152},{28,156},{32,... | collective-permute-start | bytes 122888 | tf_op jit(solution)/shard_map/ppermute | solution.py:305
  17.0 1.5 %collective-permute-done.1 = f32[20,512]{1,0:T(8,128)S(1)} collective-permute-done((f32[20,512]{1,0:T(8,128)S(1)}, f32[20,512]{1,0:T(8,128)S(1)}, u32[]{:S(2)}, u32[]{:S(2)}) %collective-permute-start.1) | collective-permute-done | bytes 40992 | tf_op jit(solution)/shard_map/ppermute | solution.py:305
  18.5 0.0 copy-start.1
  18.5 0.0 copy-start.2
  18.6 0.0 copy-start.3
  18.6 1.5 %collective-permute-start.2 = (f32[20,512]{1,0:T(8,128)S(1)}, f32[20,512]{1,0:T(8,128)S(1)}, u32[]{:S(2)}, u32[]{:S(2)}) collective-permute-start(f32[20,512]{1,0:T(8,128)S(1)} %add.23), channel_id=1, source_target_pairs={{0,8},{4,12},{8,0},{12,4},{16,80},{20,84},{24,88},{28,92},{32,40},... | collective-permute-start | bytes 122888 | tf_op jit(solution)/shard_map/ppermute | solution.py:305
  20.1 2.7 %collective-permute-done.2 = f32[20,512]{1,0:T(8,128)S(1)} collective-permute-done((f32[20,512]{1,0:T(8,128)S(1)}, f32[20,512]{1,0:T(8,128)S(1)}, u32[]{:S(2)}, u32[]{:S(2)}) %collective-permute-start.2) | collective-permute-done | bytes 40992 | tf_op jit(solution)/shard_map/ppermute | solution.py:305
  22.8 0.8 collective-permute-start.3
  23.6 0.0 all-to-all-done
  23.6 1.3 %lay.1 = (f32[8,80,512]{2,1,0:T(8,128)S(1)}, f32[80,512]{1,0:T(8,128)S(1)}, f32[80,512]{1,0:T(8,128)S(1)}, f32[80,128]{1,0:T(8,128)S(1)}, f32[80,128]{1,0:T(8,128)S(1)}) custom-call(s32[5]{0:T(128)S(1)} %stack.38.place_ref, f32[2560,128]{1,0:T(8,128)S(1)} %bitcast.14, f32[20,512]{1,0:T(8,128)S(1)} %add.24.after_ref), custom_call_target="tpu_custom_call" | custom-call | flops 2000000 | bytes 4000000 | tf_op jit(solution)/shard_map/lay/pallas_call | solution.py:309
  25.0 3.8 %collective-permute-start.9 = (f32[80,512]{1,0:T(8,128)S(1)}, f32[80,512]{1,0:T(8,128)S(1)}, u32[]{:S(2)}, u32[]{:S(2)}) collective-permute-start(f32[80,512]{1,0:T(8,128)S(1)} %get-tuple-element.29), channel_id=1, source_target_pairs={{0,16},{16,32},{32,48},{48,64},{64,80},{80,96},{96,112},{112,128},... | collective-permute-start | bytes 491528 | tf_op jit(solution)/shard_map/ppermute | solution.py:321
  28.8 1.9 %collective-permute-start.10 = (f32[80,512]{1,0:T(8,128)S(1)}, f32[80,512]{1,0:T(8,128)S(1)}, u32[]{:S(2)}, u32[]{:S(2)}) collective-permute-start(f32[80,512]{1,0:T(8,128)S(1)} %get-tuple-element.30), channel_id=1, source_target_pairs={{16,0},{32,16},{48,32},{64,48},{80,64},{96,80},{112,96},{128,112},... | collective-permute-start | bytes 491528 | tf_op jit(solution)/shard_map/ppermute | solution.py:322
  30.7 0.0 collective-permute-done.3
  30.7 1.3 %collective-permute-start.4 = (f32[20,512]{1,0:T(8,128)S(1)}, f32[20,512]{1,0:T(8,128)S(1)}, u32[]{:S(2)}, u32[]{:S(2)}) collective-permute-start(f32[20,512]{1,0:T(8,128)S(1)} %add.25), channel_id=1, source_target_pairs={{0,64},{4,68},{8,72},{12,76},{16,20},{20,16},{24,28},{28,24},{32,9... | collective-permute-start | bytes 122888 | tf_op jit(solution)/shard_map/ppermute | solution.py:305
  32.0 1.7 %collective-permute-done.4 = f32[20,512]{1,0:T(8,128)S(1)} collective-permute-done((f32[20,512]{1,0:T(8,128)S(1)}, f32[20,512]{1,0:T(8,128)S(1)}, u32[]{:S(2)}, u32[]{:S(2)}) %collective-permute-start.4) | collective-permute-done | bytes 40992 | tf_op jit(solution)/shard_map/ppermute | solution.py:305
  33.8 2.8 %collective-permute-start.5 = (f32[20,512]{1,0:T(8,128)S(1)}, f32[20,512]{1,0:T(8,128)S(1)}, u32[]{:S(2)}, u32[]{:S(2)}) collective-permute-start(f32[20,512]{1,0:T(8,128)S(1)} %add.26), channel_id=1, source_target_pairs={{0,128},{4,132},{8,136},{12,140},{16,24},{20,28},{24,16},{28,20},{... | collective-permute-start | bytes 122888 | tf_op jit(solution)/shard_map/ppermute | solution.py:305
  36.6 2.2 %collective-permute-start.11 = (f32[80,128]{1,0:T(8,128)S(1)}, f32[80,128]{1,0:T(8,128)S(1)}, u32[]{:S(2)}, u32[]{:S(2)}) collective-permute-start(f32[80,128]{1,0:T(8,128)S(1)} %get-tuple-element.31), channel_id=1, source_target_pairs={{0,4},{4,8},{8,12},{1,5},{5,9},{9,13},{2,6},{6,10},{10,14},{3,7},{... | collective-permute-start | bytes 122888 | tf_op jit(solution)/shard_map/ppermute | solution.py:323
  38.8 1.3 %collective-permute-start.12 = (f32[80,128]{1,0:T(8,128)S(1)}, f32[80,128]{1,0:T(8,128)S(1)}, u32[]{:S(2)}, u32[]{:S(2)}) collective-permute-start(f32[80,128]{1,0:T(8,128)S(1)} %get-tuple-element.32), channel_id=1, source_target_pairs={{4,0},{8,4},{12,8},{5,1},{9,5},{13,9},{6,2},{10,6},{14,10},{7,3},{... | collective-permute-start | bytes 122888 | tf_op jit(solution)/shard_map/ppermute | solution.py:324
  40.1 0.0 collective-permute-done.5
  40.2 0.4 collective-permute-start.8
  40.6 0.0 collective-permute-done.11.left_ref
  40.6 2.2 %collective-permute-start.7 = (f32[20,512]{1,0:T(8,128)S(1)}, f32[20,512]{1,0:T(8,128)S(1)}, u32[]{:S(2)}, u32[]{:S(2)}) collective-permute-start(f32[20,512]{1,0:T(8,128)S(1)} %add.27.own_ref), channel_id=1, source_target_pairs={{0,2},{1,3},{2,0},{3,1},{4,6},{5,7},{6,4},{7,5},{8,10},{9,11},{10,... | collective-permute-start | bytes 122888 | tf_op jit(solution)/shard_map/ppermute | solution.py:330
  42.8 0.8 collective-permute-done.12.right_ref
  43.6 1.6 %collective-permute-start.6 = (f32[20,512]{1,0:T(8,128)S(1)}, f32[20,512]{1,0:T(8,128)S(1)}, u32[]{:S(2)}, u32[]{:S(2)}) collective-permute-start(f32[20,512]{1,0:T(8,128)S(1)} %add.27.own_ref), channel_id=1, source_target_pairs={{0,3},{1,0},{2,1},{3,2},{4,7},{5,4},{6,5},{7,6},{8,11},{9,8},{10,9... | collective-permute-start | bytes 122888 | tf_op jit(solution)/shard_map/ppermute | solution.py:330
  45.2 0.0 collective-permute-done.8.three_ref
  45.2 0.1 collective-permute-done.7.two_ref
  45.3 1.2 %collective-permute-done.6.one_ref = f32[20,512]{1,0:T(8,128)S(1)} collective-permute-done((f32[20,512]{1,0:T(8,128)S(1)}, f32[20,512]{1,0:T(8,128)S(1)}, u32[]{:S(2)}, u32[]{:S(2)}) %collective-permute-start.6) | collective-permute-done | bytes 40992 | tf_op jit(solution)/shard_map/ppermute | solution.py:330
  46.5 0.0 collective-permute-done.9.up_ref
  46.5 0.0 collective-permute-done.10.down_ref
  46.5 11.7 %collective-permute-start.13 = (f32[4,20,512]{2,1,0:T(8,128)S(1)}, f32[4,20,512]{2,1,0:T(8,128)S(1)}, u32[]{:S(2)}, u32[]{:S(2)}) collective-permute-start(f32[4,20,512]{2,1,0:T(8,128)S(1)} %pad_maximum_fusion.after_ref), channel_id=1, source_target_pairs={{0,16},{16,0},{1,17},{17,1},{2,18},{18,2},{3,19},{19,3},{4,20},{20... | collective-permute-start | bytes 491528 | tf_op jit(solution)/shard_map/ppermute | solution.py:335
  58.2 0.0 copy-done.4
  58.2 2.6 %taper.1 = (f32[40,256,128]{2,1,0:T(8,128)S(1)}, f32[4,256,128]{2,1,0:T(8,128)S(1)}, f32[6,256,256]{2,1,0:T(8,128)S(1)}) custom-call(s32[5]{0:T(128)S(1)} %stack.38.place_ref, s32[4,3,256]{2,1,0:T(4,128)S(1)} %copy.7.where_ref, s32[4,256]{1,0:T(4,128)S(1)} %copy-done.4, f32[4,20,512]{2,1,0:T(8,128)S(1)} %pad_maximum_fusion.after_ref), custom_call_target="tpu_custom_call" | custom-call | flops 20000000 | bytes 8000000 | tf_op jit(solution)/shard_map/taper/pallas_call | solution.py:337
  60.8 0.0 collective-permute-done.13.other_ref
  60.8 0.0 copy-done.1
  60.8 0.0 copy-done.2
  60.9 0.0 copy-done.3
  60.9 16.0 %main.1 = f32[2560,128]{1,0:T(8,128)S(1)} custom-call(s32[5]{0:T(128)S(1)} %stack.38.place_ref, f32[4,256]{1,0:T(4,128)S(1)} %copy-done.2, f32[4,256]{1,0:T(4,128)S(1)} %copy-done.3, f32[20,512]{1,0:T(8,128)S(1)} %add.27.own_ref, f32[20,512]{1,0:T(8,128)S(1)} %collective-permute-done.6.one_ref, f32[20,512]{1,0:T(8,128)S(1)} %collective-permute-done.7.two_ref, ...), custom_call_target="tpu_custom_call" | custom-call | tf_op jit(solution)/shard_map/main/pallas_call | solution.py:350
  76.9 20.9 %all_to_all.10 = f32[16,20,8,128]{3,2,1,0:T(8,128)S(1)} all-to-all(f32[16,20,8,128]{3,2,1,0:T(8,128)S(1)} %bitcast.12), channel_id=1, replica_groups=mesh['gx_0'=8,'gx_1'=2,'gy'=4,'ens'=4] {'ens'}, dimensions={0} | all-to-all | bytes 2621440 | tf_op jit(solution)/shard_map/all_to_all | solution.py:370
  97.8 1.1 %copy.10 = f32[16,20,8,128]{3,2,1,0:T(8,128)} copy(f32[16,20,8,128]{3,2,1,0:T(8,128)S(1)} %all_to_all.10) | data formatting | bytes 2621440
  (9 shorter events, 0.1 us)
Async XLA Ops:
  0.0 5.3 %copy-start = (f32[16,20,8,128]{3,2,1,0:T(8,128)S(1)}, f32[16,20,8,128]{3,2,1,0:T(8,128)}, u32[]{:S(2)}) copy-start(f32[16,20,8,128]{3,2,1,0:T(8,128)} %param.6) | copy-start | bytes 3932164
  0.0 5.1 %copy-start.5 = (s32[4,3,256]{2,0,1:T(4,128)S(1)}, s32[4,3,256]{2,0,1:T(4,128)}, u32[]{:S(2)}) copy-start(s32[4,3,256]{2,0,1:T(4,128)} %param.9) | copy-start | bytes 36868
  0.0 23.6 %all-to-all-start = ((f32[16,20,8,128]{3,2,1,0:T(8,128)}), f32[16,20,8,128]{3,2,1,0:T(8,128)S(1)}, u32[]{:S(2)}, u32[]{:S(2)}) async-start(f32[16,20,8,128]{3,2,1,0:T(8,128)} %param.6), calls=%async_computation | async-start | bytes 2621440 | tf_op jit(solution)/shard_map/all_to_all | solution.py:302
  8.1 2.7 %collective-permute-start = (f32[20,512]{1,0:T(8,128)S(1)}, f32[20,512]{1,0:T(8,128)S(1)}, u32[]{:S(2)}, u32[]{:S(2)}) collective-permute-start(f32[20,512]{1,0:T(8,128)S(1)} %get-tuple-element.26), channel_id=1, source_target_pairs={{0,16},{16,0},{1,17},{17,1},{2,18},{18,2},{3,19},{19,3},{4,20},{20... | collective-permute-start | bytes 122888 | tf_op jit(solution)/shard_map/ppermute | solution.py:303
  10.8 47.4 %copy-start.4 = (s32[4,256]{1,0:T(4,128)S(1)}, s32[4,256]{1,0:T(4,128)}, u32[]{:S(2)}) copy-start(s32[4,256]{1,0:T(4,128)} %radius_ref.1) | copy-start | bytes 12292
  10.9 7.7 %collective-permute-start.1 = (f32[20,512]{1,0:T(8,128)S(1)}, f32[20,512]{1,0:T(8,128)S(1)}, u32[]{:S(2)}, u32[]{:S(2)}) collective-permute-start(f32[20,512]{1,0:T(8,128)S(1)} %add.22), channel_id=1, source_target_pairs={{0,4},{4,0},{8,12},{12,8},{16,144},{20,148},{24,152},{28,156},{32,... | collective-permute-start | bytes 122888 | tf_op jit(solution)/shard_map/ppermute | solution.py:305
  18.5 42.3 %copy-start.1 = (f32[2,16,8,128]{3,2,1,0:T(8,128)S(1)}, f32[2,16,8,128]{3,2,1,0:T(8,128)}, u32[]{:S(2)}) copy-start(f32[2,16,8,128]{3,2,1,0:T(8,128)} %wind_ref.1) | copy-start | bytes 393220
  18.5 42.3 %copy-start.2 = (f32[4,256]{1,0:T(4,128)S(1)}, f32[4,256]{1,0:T(4,128)}, u32[]{:S(2)}) copy-start(f32[4,256]{1,0:T(4,128)} %value_ref.1) | copy-start | bytes 12292
  18.6 42.3 %copy-start.3 = (f32[4,256]{1,0:T(4,128)S(1)}, f32[4,256]{1,0:T(4,128)}, u32[]{:S(2)}) copy-start(f32[4,256]{1,0:T(4,128)} %error_ref.1) | copy-start | bytes 12292
  18.6 4.2 %collective-permute-start.2 = (f32[20,512]{1,0:T(8,128)S(1)}, f32[20,512]{1,0:T(8,128)S(1)}, u32[]{:S(2)}, u32[]{:S(2)}) collective-permute-start(f32[20,512]{1,0:T(8,128)S(1)} %add.23), channel_id=1, source_target_pairs={{0,8},{4,12},{8,0},{12,4},{16,80},{20,84},{24,88},{28,92},{32,40},... | collective-permute-start | bytes 122888 | tf_op jit(solution)/shard_map/ppermute | solution.py:305
  22.8 7.9 %collective-permute-start.3 = (f32[20,512]{1,0:T(8,128)S(1)}, f32[20,512]{1,0:T(8,128)S(1)}, u32[]{:S(2)}, u32[]{:S(2)}) collective-permute-start(f32[20,512]{1,0:T(8,128)S(1)} %add.24.after_ref), channel_id=1, source_target_pairs={{0,32},{4,36},{8,40},{12,44},{16,48},{20,52},{24,56},{28,60},{32,0... | collective-permute-start | bytes 122888 | tf_op jit(solution)/shard_map/ppermute | solution.py:305
  25.0 21.5 %collective-permute-start.9 = (f32[80,512]{1,0:T(8,128)S(1)}, f32[80,512]{1,0:T(8,128)S(1)}, u32[]{:S(2)}, u32[]{:S(2)}) collective-permute-start(f32[80,512]{1,0:T(8,128)S(1)} %get-tuple-element.29), channel_id=1, source_target_pairs={{0,16},{16,32},{32,48},{48,64},{64,80},{80,96},{96,112},{112,128},... | collective-permute-start | bytes 491528 | tf_op jit(solution)/shard_map/ppermute | solution.py:321
  28.8 17.7 %collective-permute-start.10 = (f32[80,512]{1,0:T(8,128)S(1)}, f32[80,512]{1,0:T(8,128)S(1)}, u32[]{:S(2)}, u32[]{:S(2)}) collective-permute-start(f32[80,512]{1,0:T(8,128)S(1)} %get-tuple-element.30), channel_id=1, source_target_pairs={{16,0},{32,16},{48,32},{64,48},{80,64},{96,80},{112,96},{128,112},... | collective-permute-start | bytes 491528 | tf_op jit(solution)/shard_map/ppermute | solution.py:322
  30.7 3.0 %collective-permute-start.4 = (f32[20,512]{1,0:T(8,128)S(1)}, f32[20,512]{1,0:T(8,128)S(1)}, u32[]{:S(2)}, u32[]{:S(2)}) collective-permute-start(f32[20,512]{1,0:T(8,128)S(1)} %add.25), channel_id=1, source_target_pairs={{0,64},{4,68},{8,72},{12,76},{16,20},{20,16},{24,28},{28,24},{32,9... | collective-permute-start | bytes 122888 | tf_op jit(solution)/shard_map/ppermute | solution.py:305
  33.8 6.3 %collective-permute-start.5 = (f32[20,512]{1,0:T(8,128)S(1)}, f32[20,512]{1,0:T(8,128)S(1)}, u32[]{:S(2)}, u32[]{:S(2)}) collective-permute-start(f32[20,512]{1,0:T(8,128)S(1)} %add.26), channel_id=1, source_target_pairs={{0,128},{4,132},{8,136},{12,140},{16,24},{20,28},{24,16},{28,20},{... | collective-permute-start | bytes 122888 | tf_op jit(solution)/shard_map/ppermute | solution.py:305
  36.6 4.0 %collective-permute-start.11 = (f32[80,128]{1,0:T(8,128)S(1)}, f32[80,128]{1,0:T(8,128)S(1)}, u32[]{:S(2)}, u32[]{:S(2)}) collective-permute-start(f32[80,128]{1,0:T(8,128)S(1)} %get-tuple-element.31), channel_id=1, source_target_pairs={{0,4},{4,8},{8,12},{1,5},{5,9},{9,13},{2,6},{6,10},{10,14},{3,7},{... | collective-permute-start | bytes 122888 | tf_op jit(solution)/shard_map/ppermute | solution.py:323
  38.8 4.7 %collective-permute-start.12 = (f32[80,128]{1,0:T(8,128)S(1)}, f32[80,128]{1,0:T(8,128)S(1)}, u32[]{:S(2)}, u32[]{:S(2)}) collective-permute-start(f32[80,128]{1,0:T(8,128)S(1)} %get-tuple-element.32), channel_id=1, source_target_pairs={{4,0},{8,4},{12,8},{5,1},{9,5},{13,9},{6,2},{10,6},{14,10},{7,3},{... | collective-permute-start | bytes 122888 | tf_op jit(solution)/shard_map/ppermute | solution.py:324
  40.2 5.1 %collective-permute-start.8 = (f32[20,512]{1,0:T(8,128)S(1)}, f32[20,512]{1,0:T(8,128)S(1)}, u32[]{:S(2)}, u32[]{:S(2)}) collective-permute-start(f32[20,512]{1,0:T(8,128)S(1)} %add.27.own_ref), channel_id=1, source_target_pairs={{0,1},{1,2},{2,3},{3,0},{4,5},{5,6},{6,7},{7,4},{8,9},{9,10},{10,1... | collective-permute-start | bytes 122888 | tf_op jit(solution)/shard_map/ppermute | solution.py:330
  40.6 4.7 %collective-permute-start.7 = (f32[20,512]{1,0:T(8,128)S(1)}, f32[20,512]{1,0:T(8,128)S(1)}, u32[]{:S(2)}, u32[]{:S(2)}) collective-permute-start(f32[20,512]{1,0:T(8,128)S(1)} %add.27.own_ref), channel_id=1, source_target_pairs={{0,2},{1,3},{2,0},{3,1},{4,6},{5,7},{6,4},{7,5},{8,10},{9,11},{10,... | collective-permute-start | bytes 122888 | tf_op jit(solution)/shard_map/ppermute | solution.py:330
  43.6 2.9 %collective-permute-start.6 = (f32[20,512]{1,0:T(8,128)S(1)}, f32[20,512]{1,0:T(8,128)S(1)}, u32[]{:S(2)}, u32[]{:S(2)}) collective-permute-start(f32[20,512]{1,0:T(8,128)S(1)} %add.27.own_ref), channel_id=1, source_target_pairs={{0,3},{1,0},{2,1},{3,2},{4,7},{5,4},{6,5},{7,6},{8,11},{9,8},{10,9... | collective-permute-start | bytes 122888 | tf_op jit(solution)/shard_map/ppermute | solution.py:330
  46.5 14.3 %collective-permute-start.13 = (f32[4,20,512]{2,1,0:T(8,128)S(1)}, f32[4,20,512]{2,1,0:T(8,128)S(1)}, u32[]{:S(2)}, u32[]{:S(2)}) collective-permute-start(f32[4,20,512]{2,1,0:T(8,128)S(1)} %pad_maximum_fusion.after_ref), channel_id=1, source_target_pairs={{0,16},{16,0},{1,17},{17,1},{2,18},{18,2},{3,19},{19,3},{4,20},{20... | collective-permute-start | bytes 491528 | tf_op jit(solution)/shard_map/ppermute | solution.py:335
where the time goes:
time: 99.1 us; the launch traced here: 98.8 us
  starting transfers between devices  44.8 us (45%)
  Pallas kernels  22.9 us (23%)
  blocking collectives  20.9 us (21%)
  waiting for transfers between devices  8.9 us (9%)
  local copies, waits for them, and re-layouts  1.18 us (1%)
    all_to_all x1, blocking collectives, shards(): return lax.all_to_all(out, 'ens', split_axis=0, concat_axis=0, tiled=True)  20.9 us
    pallas_call x1, Pallas kernels, shards(): pl.pallas_call(main_kernel, out_shape=jax.ShapeDtypeStruct((flat, tile_co...  16 us
    ppermute x5, starting transfers between devices, shards(): got = lax.ppermute(x, (*GX, 'gy'), pairs)  12.7 us
    ppermute x1, starting transfers between devices, shards(): other = lax.ppermute(stacked, 'gx_1', ring('gx_1', 1))  11.7 us
    ppermute x5, waiting for transfers between devices, shards(): got = lax.ppermute(x, (*GX, 'gy'), pairs)  5.91 us
    all_to_all x1, starting transfers between devices, shards(): cur = lax.all_to_all(state, 'ens', split_axis=0, concat_axis=0, tiled=True)  5.13 us
    ppermute x3, starting transfers between devices, shards(): gathered.append(lax.ppermute(own, 'ens', ring('ens', -k)))  4.26 us
    ppermute x1, starting transfers between devices, shards(): up = lax.ppermute(low, GX, line(GX, 1))  3.8 us
  transfers between devices with their start and end apart: 15, of which 7 were waited for; matrix products, arithmetic and copies ran while one was open for 0% of the time, Pallas kernels for 7%

commit v1 on v0

--- a/solution.py
+++ b/solution.py
@@ -12,7 +12,7 @@
 DIFFUSE = 0.05
 F32 = jnp.float32
 BF16 = jnp.bfloat16
-ROWS = 2
+ROWS = 5
 VMEM = pltpu.VMEM
 SMEM = pltpu.SMEM
 
@@ -58,6 +58,13 @@
             out_ref[:, at * n_obs : (at + 1) * n_obs] = total
 
 
+def stack_kernel(own_ref, one_ref, two_ref, three_ref, inner_ref, out_ref):
+    size = own_ref.shape[0]
+    for at, ref in enumerate((own_ref, one_ref, two_ref, three_ref)):
+        out_ref[at * size : (at + 1) * size, :] = ref[...]
+    out_ref[4 * size :, :] = inner_ref[...]
+
+
 def taper(dist_sq, reach):
     weight = jnp.maximum(0.0, 1.0 - dist_sq * reach)
     return weight * weight
@@ -71,7 +78,7 @@
     return jnp.concatenate([block] * (lanes // 128), axis=1)
 
 
-def lay_kernel(place_ref, cur_ref, after_ref, y_ref, top_ref, low_ref, left_ref, right_ref):
+def lay_kernel(place_ref, cur_ref, after_ref, y_ref, far_ref, near_ref, left_ref, right_ref):
     me = place_ref[3]
     cols = cur_ref.shape[1]
     shares = 4
@@ -84,8 +91,9 @@
             for row in range(8):
                 got = cur_ref[pl.ds(base + row, members, stride=8), :]
                 y_ref[row, share * members : (share + 1) * members, level * cols : (level + 1) * cols] = got
-    top_ref[...] = y_ref[0]
-    low_ref[...] = y_ref[7]
+    core = place_ref[2]
+    far_ref[...] = y_ref[7 * core]
+    near_ref[...] = y_ref[7 * (1 - core)]
     lane = lax.broadcasted_iota(jnp.int32, left_ref.shape, 1)
     left = jnp.zeros(left_ref.shape, F32)
     right = jnp.zeros(left_ref.shape, F32)
@@ -142,27 +150,81 @@
     return outs
 
 
-def main_kernel(
-    place_ref, value_ref, error_ref, own_ref, one_ref, two_ref, three_ref, other_ref,
-    y_ref, up_ref, down_ref, left_ref, right_ref, w_ref, wc_ref, wo_ref, wind_ref,
-    out_ref, prior_ref, z_ref, edge_ref, s3_ref, n2_ref, f_ref,
+def posterior(z_ref, w_ref, batch, s3, n2):
+    def step(at, carry):
+        rows = [ROWS * at + k for k in range(ROWS)]
+        xs = [z_ref[row] for row in rows]
+        ws = [wide(w_ref[batch * 10 + row], z_ref.shape[2]) for row in rows]
+        for row, out in zip(rows, changed(xs, ws, s3, n2)):
+            z_ref[row] = out
+        return carry
+
+    lax.fori_loop(0, 10 // ROWS, step, 0)
+
+
+def take_rows(span, place_ref, y_ref, far_ref, pack_ref, z_ref):
+    core = place_ref[2]
+    members = z_ref.shape[1]
+    z_ref[9 * core] = far_ref[:, span]
+    z_ref[9 * (1 - core)] = pack_ref[members:, span]
+    for row in range(8):
+        z_ref[row + 1] = y_ref[row, :, span]
+
+
+def transported(first, place_ref, z_ref, edge_ref, wind_ref, f_ref, out_refs):
+    lev_start = place_ref[4]
+    members = z_ref.shape[1]
+    cols = edge_ref.shape[1]
+    levels = z_ref.shape[2] // cols
+    share_size = members // len(out_refs)
+    lane = lax.broadcasted_iota(jnp.int32, (members, cols), 1)
+
+    def transport(row, carry):
+        edge = edge_ref[...]
+        for level in range(levels):
+            span = slice(level * cols, (level + 1) * cols)
+            a = wind_ref[0, lev_start + first + level, pl.ds(row, 1), :]
+            b = wind_ref[1, lev_start + first + level, pl.ds(row, 1), :]
+            to_up = jnp.maximum(a, 0.0) + DIFFUSE
+            to_down = DIFFUSE - jnp.minimum(a, 0.0)
+            to_left = jnp.maximum(b, 0.0) + DIFFUSE
+            to_right = DIFFUSE - jnp.minimum(b, 0.0)
+            stay = 1.0 - ((to_up + to_down) + (to_left + to_right))
+            x = z_ref[row + 1, :, span]
+            at = (first + level) * 8 + row
+            left = jnp.where(lane == 0, pltpu.roll(edge, lax.rem(cols - at, cols), 1), pltpu.roll(x, 1, 1))
+            right = jnp.where(
+                lane == cols - 1, pltpu.roll(edge, cols - 33 - at, 1), pltpu.roll(x, cols - 1, 1)
+            )
+            f_ref[level] = (
+                stay * x + to_up * z_ref[row, :, span] + to_down * z_ref[row + 2, :, span]
+                + to_left * left + to_right * right
+            )
+            for share, out_ref in enumerate(out_refs):
+                out_ref[pl.ds(level * share_size * 8 + row, share_size, stride=8), :] = f_ref[
+                    level, share * share_size : (share + 1) * share_size, :
+                ]
+        return carry
+
+    lax.fori_loop(0, 8, transport, 0)
+
+
+def first_kernel(
+    place_ref, value_ref, error_ref, own_ref, one_ref, two_ref, three_ref, pack_ref,
+    y_ref, far_ref, left_ref, right_ref, w_ref, wc_ref, wo_ref, wind_ref,
+    out0_ref, out1_ref, out2_ref, out3_ref, s3_ref, n2_ref, edge_ref, prior_ref, z_ref, f_ref,
 ):
-    core, me, lev_start = place_ref[2], place_ref[3], place_ref[4]
+    core = place_ref[2]
     batches, n_obs = value_ref.shape
     members = z_ref.shape[1]
     shares = 4
     share_size = members // shares
-    cols = w_ref.shape[2]
-    levels = z_ref.shape[2] // cols
     half = own_ref.shape[1]
     for share, ref in enumerate((own_ref, one_ref, two_ref, three_ref)):
         rows = slice(share * share_size, (share + 1) * share_size)
         prior_ref[core, rows, :] = ref[...]
-        prior_ref[1 - core, rows, :] = other_ref[share]
-    z_ref[0] = up_ref[...]
-    z_ref[9] = down_ref[...]
-    for row in range(8):
-        z_ref[row + 1] = y_ref[row]
+    prior_ref[1 - core] = pack_ref[:members]
+    take_rows(slice(0, z_ref.shape[2]), place_ref, y_ref, far_ref, pack_ref, z_ref)
     edge_ref[...] = left_ref[...] + right_ref[...]
     per_half = half // n_obs
 
@@ -183,63 +245,49 @@
         nudges = post_mean + factor * spread - priors
         inverse = 1.0 / ((members - 1) * (variance + EPSILON))
         n_high, n_low = split(nudges * inverse)
-        n2_ref[...] = jnp.concatenate([n_high, n_low], axis=0)
+        n2 = jnp.concatenate([n_high, n_low], axis=0)
         s_high, s_low = split(spread)
         s3 = jnp.concatenate([s_high.astype(F32), s_low.astype(F32), s_high.astype(F32)], axis=0)
-        s3_ref[...] = jnp.transpose(s3).astype(BF16)
+        s3 = jnp.transpose(s3).astype(BF16)
+        n2_ref[batch] = n2
+        s3_ref[batch] = s3
         laters = range(batch + 1, batches)
         first = batch * (2 * batches - batch - 1) // 2
         blocks = [edge_ref[...]] + [prior_ref[lanes(k)[0], :, lanes(k)[1]] for k in laters]
         tapers = [wc_ref[batch]] + [wo_ref[first + k] for k in range(len(laters))]
-        blocks = changed(blocks, tapers, s3_ref[...], n2_ref[...])
+        blocks = changed(blocks, tapers, s3, n2)
         edge_ref[...] = blocks[0]
         for k, block in zip(laters, blocks[1:]):
             prior_ref[lanes(k)[0], :, lanes(k)[1]] = block
-
-        def step(at, carry):
-            rows = [ROWS * at + k for k in range(ROWS)]
-            xs = [z_ref[row, :, k * 256 : (k + 1) * 256] for row in rows for k in range(2)]
-            ws = [wide(w_ref[batch * 10 + row], 256) for row in rows for _ in range(2)]
-            outs = changed(xs, ws, s3_ref[...], n2_ref[...])
-            for at_out, out in enumerate(outs):
-                k = at_out % 2
-                z_ref[rows[at_out // 2], :, k * 256 : (k + 1) * 256] = out
-            return carry
-
-        lax.fori_loop(0, 10 // ROWS, step, 0)
-
-    lane = lax.broadcasted_iota(jnp.int32, (members, cols), 1)
-
-    def transport(row, carry):
-        edge = edge_ref[...]
-        for level in range(levels):
-            span = slice(level * cols, (level + 1) * cols)
-            a = wind_ref[0, lev_start + level, pl.ds(row, 1), :]
-            b = wind_ref[1, lev_start + level, pl.ds(row, 1), :]
-            to_up = jnp.maximum(a, 0.0) + DIFFUSE
-            to_down = DIFFUSE - jnp.minimum(a, 0.0)
-            to_left = jnp.maximum(b, 0.0) + DIFFUSE
-            to_right = DIFFUSE - jnp.minimum(b, 0.0)
-            stay = 1.0 - ((to_up + to_down) + (to_left + to_right))
-            x = z_ref[row + 1, :, span]
-            at = level * 8 + row
-            left = jnp.where(lane == 0, pltpu.roll(edge, lax.rem(cols - at, cols), 1), pltpu.roll(x, 1, 1))
-            right = jnp.where(
-                lane == cols - 1, pltpu.roll(edge, cols - 33 - at, 1), pltpu.roll(x, cols - 1, 1)
-            )
-            f_ref[...] = (
-                stay * x + to_up * z_ref[row, :, span] + to_down * z_ref[row + 2, :, span]
-                + to_left * left + to_right * right
-            )
-            for share in range(shares):
-                target = lax.rem(me + share, shares)
-                base = (target * levels + level) * share_size * 8
-                out_ref[pl.ds(base + row, share_size, stride=8), :] = f_ref[
-                    share * share_size : (share + 1) * share_size, :
-                ]
-        return carry
-
-    lax.fori_loop(0, 8, transport, 0)
+        posterior(z_ref, w_ref, batch, s3_ref[batch], n2_ref[batch])
+    transported(0, place_ref, z_ref, edge_ref, wind_ref, f_ref, (out0_ref, out1_ref, out2_ref, out3_ref))
+
+
+def second_kernel(
+    place_ref, pack_ref, y_ref, far_ref, s3_ref, n2_ref, edge_ref, w_ref, wind_ref,
+    out0_ref, out1_ref, out2_ref, out3_ref, z_ref, f_ref,
+):
+    width = z_ref.shape[2]
+    first = width // edge_ref.shape[1]
+    take_rows(slice(width, 2 * width), place_ref, y_ref, far_ref, pack_ref, z_ref)
+    for batch in range(s3_ref.shape[0]):
+        posterior(z_ref, w_ref, batch, s3_ref[batch], n2_ref[batch])
+    transported(first, place_ref, z_ref, edge_ref, wind_ref, f_ref, (out0_ref, out1_ref, out2_ref, out3_ref))
+
+
+def place_kernel(place_ref, *refs):
+    blocks, out_ref, sems = refs[:8], refs[8], refs[9]
+    me = place_ref[3]
+    length = blocks[0].shape[0]
+    copies = []
+    for at, block in enumerate(blocks):
+        source = lax.rem(me + 4 - at % 4, 4)
+        start = pl.multiple_of((source * 2 + at // 4) * length, length)
+        copies.append(pltpu.make_async_copy(block, out_ref.at[pl.ds(start, length)], sems.at[at]))
+    for copy in copies:
+        copy.start()
+    for copy in copies:
+        copy.wait()
 
 
 def ring(axis, shift):
@@ -250,6 +298,11 @@
 def line(axis, shift):
     n = lax.axis_size(axis)
     return [(i, i + shift) for i in range(n) if 0 <= i + shift < n]
+
+
+def beyond():
+    n = lax.axis_size(GX)
+    return [(i, i - 1) for i in range(2, n, 2)] + [(i, i + 1) for i in range(1, n - 1, 2)]
 
 
 def exchanges():
@@ -306,7 +359,7 @@
         if step == 3:
             line_shape = jax.ShapeDtypeStruct((members, here * tile_cols), F32)
             edge_shape = jax.ShapeDtypeStruct((members, tile_cols), F32)
-            y, top, low, left, right = pl.pallas_call(
+            y, outer, inner, left, right = pl.pallas_call(
                 lay_kernel,
                 out_shape=[
                     jax.ShapeDtypeStruct((tile_rows, members, here * tile_cols), F32),
@@ -318,8 +371,7 @@
                 cost_estimate=pl.CostEstimate(flops=2_000_000, bytes_accessed=4_000_000, transcendentals=0),
                 name="lay",
             )(place, cur.reshape(flat, tile_cols), x)
-            up = lax.ppermute(low, GX, line(GX, 1))
-            down_ = lax.ppermute(top, GX, line(GX, -1))
+            far = lax.ppermute(outer, GX, beyond())
             from_left = lax.ppermute(right, "gy", line("gy", 1))
             from_right = lax.ppermute(left, "gy", line("gy", -1))
             got, y = lax.optimization_barrier((got, y))
@@ -328,11 +380,16 @@
     gathered = [own]
     for k in (1, 2, 3):
         gathered.append(lax.ppermute(own, "ens", ring("ens", -k)))
-    own, one, two, three, up, down_, from_left, from_right = lax.optimization_barrier(
-        (*gathered, up, down_, from_left, from_right)
-    )
-    stacked = jnp.stack([own, one, two, three])
-    other = lax.ppermute(stacked, "gx_1", ring("gx_1", 1))
+    own, one, two, three, far, from_left, from_right = lax.optimization_barrier((*gathered, far, from_left, from_right))
+    stacked = pl.pallas_call(
+        stack_kernel,
+        out_shape=jax.ShapeDtypeStruct((2 * members, half), F32),
+        in_specs=[vmem] * 5,
+        out_specs=vmem,
+        compiler_params=pltpu.CompilerParams(vmem_limit_bytes=4 << 20),
+        name="stack",
+    )(own, one, two, three, inner)
+    pack = lax.ppermute(stacked, "gx_1", ring("gx_1", 1))
     pairs = batches * (batches - 1) // 2
     w, wc, wo = pl.pallas_call(
         taper_kernel,
@@ -347,27 +404,53 @@
         cost_estimate=pl.CostEstimate(flops=20_000_000, bytes_accessed=8_000_000, transcendentals=0),
         name="taper",
     )(place, obs_where, radius, stacked)
+    width = here // 2 * tile_cols
+    piece = jax.ShapeDtypeStruct((flat // 8, tile_cols), F32)
+    scratch = [VMEM((tile_rows + 2, members, width), F32), VMEM((here // 2, members, tile_cols), F32)]
+    *early, s3, n2, edge = pl.pallas_call(
+        first_kernel,
+        out_shape=[
+            piece, piece, piece, piece,
+            jax.ShapeDtypeStruct((batches, n_obs, 3 * members), BF16),
+            jax.ShapeDtypeStruct((batches, 2 * members, n_obs), BF16),
+            edge_shape,
+        ],
+        in_specs=[smem] + [vmem] * 15,
+        out_specs=[vmem] * 7,
+        scratch_shapes=[VMEM((2, members, half), F32), *scratch],
+        compiler_params=pltpu.CompilerParams(vmem_limit_bytes=24 << 20),
+        cost_estimate=pl.CostEstimate(flops=3_000_000_000, bytes_accessed=8_000_000, transcendentals=0),
+        name="first",
+    )(
+        place, obs_value, obs_error, own, one, two, three, pack,
+        y, far, from_left, from_right, w, wc, wo, wind,
+    )
+    back = [early[0]]
+    for k in (1, 2, 3):
+        back.append(lax.ppermute(early[k], "ens", ring("ens", k)))
+    late = pl.pallas_call(
+        second_kernel,
+        out_shape=[piece] * 4,
+        in_specs=[smem] + [vmem] * 8,
+        out_specs=[vmem] * 4,
+        scratch_shapes=scratch,
+        compiler_params=pltpu.CompilerParams(vmem_limit_bytes=24 << 20),
+        cost_estimate=pl.CostEstimate(flops=3_000_000_000, bytes_accessed=8_000_000, transcendentals=0),
+        name="second",
+    )(place, pack, y, far, s3, n2, edge, w, wind)
+    back.append(late[0])
+    for k in (1, 2, 3):
+        back.append(lax.ppermute(late[k], "ens", ring("ens", k)))
     out = pl.pallas_call(
-        main_kernel,
+        place_kernel,
         out_shape=jax.ShapeDtypeStruct((flat, tile_cols), F32),
-        in_specs=[smem] + [vmem] * 16,
-        out_specs=vmem,
-        scratch_shapes=[
-            VMEM((2, members, half), F32),
-            VMEM((tile_rows + 2, members, here * tile_cols), F32),
-            VMEM((members, tile_cols), F32),
-            VMEM((n_obs, 3 * members), BF16),
-            VMEM((2 * members, n_obs), BF16),
-            VMEM((members, tile_cols), F32),
-        ],
-        compiler_params=pltpu.CompilerParams(vmem_limit_bytes=32 << 20),
-        name="main",
-    )(
-        place, obs_value, obs_error, own, one, two, three, other,
-        y, up, down_, from_left, from_right, w, wc, wo, wind,
-    )
-    out = out.reshape(levels, share_size, tile_rows, tile_cols)
-    return lax.all_to_all(out, "ens", split_axis=0, concat_axis=0, tiled=True)
+        in_specs=[smem] + [vmem] * 8,
+        out_specs=any_,
+        scratch_shapes=[pltpu.SemaphoreType.DMA((8,))],
+        compiler_params=pltpu.CompilerParams(vmem_limit_bytes=8 << 20),
+        name="place",
+    )(place, *back)
+    return out.reshape(levels, share_size, tile_rows, tile_cols)
 
 
 def solution(mesh):
@@ -377,6 +460,4 @@
     )
     placed = (P(None, "ens", GX, "gy"), P(), P(), P(), P(), P(None, None, GX, "gy"))
 
-    return jax.shard_map(
-        shards, mesh=torus, in_specs=placed, out_specs=P(None, "ens", GX, "gy"), check_vma=False
-    )
+    return jax.shard_map(shards, mesh=torus, in_specs=placed, out_specs=P(None, "ens", GX, "gy"), check_vma=False)

time: 99.1 us -> 88.9 us (0.90)
  the two profiles are of different devices: /device:TPU:1 before, /device:TPU:11 now
where the time goes in v1:
time: 88.9 us; the launch traced here: 88.7 us
  starting transfers between devices  44.1 us (50%)
  Pallas kernels  24.6 us (28%)
  waiting for transfers between devices  19.5 us (22%)
    ppermute x5, starting transfers between devices, shards(): got = lax.ppermute(x, (*GX, 'gy'), pairs)  11.9 us
    ppermute x3, waiting for transfers between devices, shards(): back.append(lax.ppermute(late[k], 'ens', ring('ens', k)))  9.37 us
    pallas_call x1, Pallas kernels, shards(): pl.pallas_call(first_kernel, out_shape=[piece, piece, piece, piece, jax.S...  9.07 us
    ppermute x1, starting transfers between devices, shards(): pack = lax.ppermute(stacked, 'gx_1', ring('gx_1', 1))  8.9 us
    pallas_call x1, Pallas kernels, shards(): pl.pallas_call(second_kernel, out_shape=[piece] * 4, in_specs=[smem] + [v...  6.93 us
    ppermute x5, waiting for transfers between devices, shards(): got = lax.ppermute(x, (*GX, 'gy'), pairs)  6.57 us
    ppermute x3, starting transfers between devices, shards(): back.append(lax.ppermute(early[k], 'ens', ring('ens', k)))  4.58 us
    all_to_all x1, starting transfers between devices, shards(): cur = lax.all_to_all(state, 'ens', split_axis=0, concat_axis=0, tiled=True)  4.48 us
  transfers between devices with their start and end apart: 20, of which 9 were waited for; matrix products, arithmetic and copies ran while one was open for 0% of the time, Pallas kernels for 16%

profile of v1, /device:TPU:11, one launch (start us, length us, event | category | flops | bytes accessed | tf_op | source)
XLA Modules:
  0.0 88.7 jit_solution(18353245199346043512)
XLA Ops:
  0.0 4.5 %all-to-all-start = ((f32[16,20,8,128]{3,2,1,0:T(8,128)}), f32[16,20,8,128]{3,2,1,0:T(8,128)S(1)}, u32[]{:S(2)}, u32[]{:S(2)}) async-start(f32[16,20,8,128]{3,2,1,0:T(8,128)} %param.6), calls=%async_computation | async-start | bytes 2621440 | tf_op jit(solution)/shard_map/all_to_all | solution.py:355
  4.5 0.1 stack.24.place_ref
  4.6 2.9 %pick.1 = (f32[20,512]{1,0:T(8,128)S(1)}, f32[20,512]{1,0:T(8,128)S(1)}) custom-call(s32[5]{0:T(128)S(1)} %stack.24.place_ref, s32[4,3,256]{2,1,0:T(4,128)S(1)} %copy.7.where_ref, f32[2560,128]{1,0:T(8,128)S(1)} %bitcast.8), custom_call_target="tpu_custom_call" | custom-call | tf_op jit(solution)/shard_map/pick/pallas_call | solution.py:345
  7.5 1.3 %collective-permute-start = (f32[20,512]{1,0:T(8,128)S(1)}, f32[20,512]{1,0:T(8,128)S(1)}, u32[]{:S(2)}, u32[]{:S(2)}) collective-permute-start(f32[20,512]{1,0:T(8,128)S(1)} %get-tuple-element.36), channel_id=1, source_target_pairs={{0,16},{16,0},{1,17},{17,1},{2,18},{18,2},{3,19},{19,3},{4,20},{20... | collective-permute-start | bytes 122888 | tf_op jit(solution)/shard_map/ppermute | solution.py:356
  8.8 0.9 collective-permute-done
  9.7 7.0 %collective-permute-start.1 = (f32[20,512]{1,0:T(8,128)S(1)}, f32[20,512]{1,0:T(8,128)S(1)}, u32[]{:S(2)}, u32[]{:S(2)}) collective-permute-start(f32[20,512]{1,0:T(8,128)S(1)} %add.22), channel_id=1, source_target_pairs={{0,4},{4,0},{8,12},{12,8},{16,144},{20,148},{24,152},{28,156},{32,... | collective-permute-start | bytes 122888 | tf_op jit(solution)/shard_map/ppermute | solution.py:358
  16.7 1.5 %collective-permute-done.1 = f32[20,512]{1,0:T(8,128)S(1)} collective-permute-done((f32[20,512]{1,0:T(8,128)S(1)}, f32[20,512]{1,0:T(8,128)S(1)}, u32[]{:S(2)}, u32[]{:S(2)}) %collective-permute-start.1) | collective-permute-done | bytes 40992 | tf_op jit(solution)/shard_map/ppermute | solution.py:358
  18.2 0.0 copy-start.1
  18.2 1.5 %collective-permute-start.2 = (f32[20,512]{1,0:T(8,128)S(1)}, f32[20,512]{1,0:T(8,128)S(1)}, u32[]{:S(2)}, u32[]{:S(2)}) collective-permute-start(f32[20,512]{1,0:T(8,128)S(1)} %add.23), channel_id=1, source_target_pairs={{0,8},{4,12},{8,0},{12,4},{16,80},{20,84},{24,88},{28,92},{32,40},... | collective-permute-start | bytes 122888 | tf_op jit(solution)/shard_map/ppermute | solution.py:358
  19.7 2.4 %collective-permute-done.2 = f32[20,512]{1,0:T(8,128)S(1)} collective-permute-done((f32[20,512]{1,0:T(8,128)S(1)}, f32[20,512]{1,0:T(8,128)S(1)}, u32[]{:S(2)}, u32[]{:S(2)}) %collective-permute-start.2) | collective-permute-done | bytes 40992 | tf_op jit(solution)/shard_map/ppermute | solution.py:358
  22.1 1.1 %collective-permute-start.3 = (f32[20,512]{1,0:T(8,128)S(1)}, f32[20,512]{1,0:T(8,128)S(1)}, u32[]{:S(2)}, u32[]{:S(2)}) collective-permute-start(f32[20,512]{1,0:T(8,128)S(1)} %add.24.after_ref), channel_id=1, source_target_pairs={{0,32},{4,36},{8,40},{12,44},{16,48},{20,52},{24,56},{28,60},{32,0... | collective-permute-start | bytes 122888 | tf_op jit(solution)/shard_map/ppermute | solution.py:358
  23.2 0.0 all-to-all-done
  23.2 1.4 %lay.1 = (f32[8,80,512]{2,1,0:T(8,128)S(1)}, f32[80,512]{1,0:T(8,128)S(1)}, f32[80,512]{1,0:T(8,128)S(1)}, f32[80,128]{1,0:T(8,128)S(1)}, f32[80,128]{1,0:T(8,128)S(1)}) custom-call(s32[5]{0:T(128)S(1)} %stack.24.place_ref, f32[2560,128]{1,0:T(8,128)S(1)} %bitcast.9, f32[20,512]{1,0:T(8,128)S(1)} %add.24.after_ref), custom_call_target="tpu_custom_call" | custom-call | flops 2000000 | bytes 4000000 | tf_op jit(solution)/shard_map/lay/pallas_call | solution.py:362
  24.7 2.4 %collective-permute-start.9 = (f32[80,512]{1,0:T(8,128)S(1)}, f32[80,512]{1,0:T(8,128)S(1)}, u32[]{:S(2)}, u32[]{:S(2)}) collective-permute-start(f32[80,512]{1,0:T(8,128)S(1)} %get-tuple-element.39), channel_id=1, source_target_pairs={{32,16},{64,48},{96,80},{128,112},{160,144},{192,176},{224,208},{1... | collective-permute-start | bytes 491528 | tf_op jit(solution)/shard_map/ppermute | solution.py:374
  27.1 0.0 collective-permute-done.3
  27.1 0.3 collective-permute-start.4
  27.4 2.7 %collective-permute-done.4 = f32[20,512]{1,0:T(8,128)S(1)} collective-permute-done((f32[20,512]{1,0:T(8,128)S(1)}, f32[20,512]{1,0:T(8,128)S(1)}, u32[]{:S(2)}, u32[]{:S(2)}) %collective-permute-start.4) | collective-permute-done | bytes 40992 | tf_op jit(solution)/shard_map/ppermute | solution.py:358
  30.1 1.9 %collective-permute-start.5 = (f32[20,512]{1,0:T(8,128)S(1)}, f32[20,512]{1,0:T(8,128)S(1)}, u32[]{:S(2)}, u32[]{:S(2)}) collective-permute-start(f32[20,512]{1,0:T(8,128)S(1)} %add.26), channel_id=1, source_target_pairs={{0,128},{4,132},{8,136},{12,140},{16,24},{20,28},{24,16},{28,20},{... | collective-permute-start | bytes 122888 | tf_op jit(solution)/shard_map/ppermute | solution.py:358
  32.1 1.9 %collective-permute-start.10 = (f32[80,128]{1,0:T(8,128)S(1)}, f32[80,128]{1,0:T(8,128)S(1)}, u32[]{:S(2)}, u32[]{:S(2)}) collective-permute-start(f32[80,128]{1,0:T(8,128)S(1)} %get-tuple-element.40), channel_id=1, source_target_pairs={{0,4},{4,8},{8,12},{1,5},{5,9},{9,13},{2,6},{6,10},{10,14},{3,7},{... | collective-permute-start | bytes 122888 | tf_op jit(solution)/shard_map/ppermute | solution.py:375
  34.0 3.4 %collective-permute-start.11 = (f32[80,128]{1,0:T(8,128)S(1)}, f32[80,128]{1,0:T(8,128)S(1)}, u32[]{:S(2)}, u32[]{:S(2)}) collective-permute-start(f32[80,128]{1,0:T(8,128)S(1)} %get-tuple-element.41), channel_id=1, source_target_pairs={{4,0},{8,4},{12,8},{5,1},{9,5},{13,9},{6,2},{10,6},{14,10},{7,3},{... | collective-permute-start | bytes 122888 | tf_op jit(solution)/shard_map/ppermute | solution.py:376
  37.4 0.0 collective-permute-done.5
  37.4 0.6 collective-permute-start.8
  38.0 2.5 %collective-permute-start.7 = (f32[20,512]{1,0:T(8,128)S(1)}, f32[20,512]{1,0:T(8,128)S(1)}, u32[]{:S(2)}, u32[]{:S(2)}) collective-permute-start(f32[20,512]{1,0:T(8,128)S(1)} %add.27.own_ref), channel_id=1, source_target_pairs={{0,2},{1,3},{2,0},{3,1},{4,6},{5,7},{6,4},{7,5},{8,10},{9,11},{10,... | collective-permute-start | bytes 122888 | tf_op jit(solution)/shard_map/ppermute | solution.py:382
  40.4 0.0 collective-permute-done.10.left_ref
  40.4 0.3 collective-permute-start.6
  40.7 0.0 collective-permute-done.11.right_ref
  40.7 0.0 collective-permute-done.8.three_ref
  40.7 1.7 %collective-permute-done.7.two_ref = f32[20,512]{1,0:T(8,128)S(1)} collective-permute-done((f32[20,512]{1,0:T(8,128)S(1)}, f32[20,512]{1,0:T(8,128)S(1)}, u32[]{:S(2)}, u32[]{:S(2)}) %collective-permute-start.7) | collective-permute-done | bytes 40992 | tf_op jit(solution)/shard_map/ppermute | solution.py:382
  42.4 0.9 %collective-permute-done.6.one_ref = f32[20,512]{1,0:T(8,128)S(1)} collective-permute-done((f32[20,512]{1,0:T(8,128)S(1)}, f32[20,512]{1,0:T(8,128)S(1)}, u32[]{:S(2)}, u32[]{:S(2)}) %collective-permute-start.6) | collective-permute-done | bytes 40992 | tf_op jit(solution)/shard_map/ppermute | solution.py:382
  43.4 0.0 collective-permute-done.9.far_ref
  43.4 8.9 %collective-permute-start.12 = (f32[160,512]{1,0:T(8,128)S(1)}, f32[160,512]{1,0:T(8,128)S(1)}, u32[]{:S(2)}, u32[]{:S(2)}) collective-permute-start(f32[160,512]{1,0:T(8,128)S(1)} %stack.25.after_ref), channel_id=1, source_target_pairs={{0,16},{16,0},{1,17},{17,1},{2,18},{18,2},{3,19},{19,3},{4,20},{20... | collective-permute-start | bytes 983048 | tf_op jit(solution)/shard_map/ppermute | solution.py:392
  52.3 2.6 %taper.1 = (f32[40,256,128]{2,1,0:T(8,128)S(1)}, f32[4,256,128]{2,1,0:T(8,128)S(1)}, f32[6,256,256]{2,1,0:T(8,128)S(1)}) custom-call(s32[5]{0:T(128)S(1)} %stack.24.place_ref, s32[4,3,256]{2,1,0:T(4,128)S(1)} %copy.7.where_ref, s32[4,256]{1,0:T(4,128)S(1)} %copy-done.1, f32[160,512]{1,0:T(8,128)S(1)} %stack.25.after_ref), custom_call_target="tpu_custom_call" | custom-call | flops 20000000 | bytes 8000000 | tf_op jit(solution)/shard_map/taper/pallas_call | solution.py:394
  54.9 0.0 collective-permute-done.12.pack_ref
  55.0 9.1 %first.1 = (f32[320,128]{1,0:T(8,128)S(1)}, f32[320,128]{1,0:T(8,128)S(1)}, f32[320,128]{1,0:T(8,128)S(1)}, f32[320,128]{1,0:T(8,128)S(1)}, bf16[4,256,240]{2,1,...) custom-call(s32[5]{0:T(128)S(1)} %stack.24.place_ref, f32[4,256]{1,0:T(4,128)S(1)} %copy-done.3, ...), custom_call_target="tpu_custom_call" | custom-call | flops 3000000000 | bytes 8000000 | tf_op jit(solution)/shard_map/first/pallas_call | solution.py:410
  64.0 0.7 collective-permute-start.13
  64.8 2.4 %collective-permute-start.14 = (f32[320,128]{1,0:T(8,128)S(1)}, f32[320,128]{1,0:T(8,128)S(1)}, u32[]{:S(2)}, u32[]{:S(2)}) collective-permute-start(f32[320,128]{1,0:T(8,128)S(1)} %get-tuple-element.56), channel_id=1, source_target_pairs={{0,2},{1,3},{2,0},{3,1},{4,6},{5,7},{6,4},{7,5},{8,10},{9,11},{10,... | collective-permute-start | bytes 491528 | tf_op jit(solution)/shard_map/ppermute | solution.py:430
  67.1 1.5 %collective-permute-start.15 = (f32[320,128]{1,0:T(8,128)S(1)}, f32[320,128]{1,0:T(8,128)S(1)}, u32[]{:S(2)}, u32[]{:S(2)}) collective-permute-start(f32[320,128]{1,0:T(8,128)S(1)} %get-tuple-element.57), channel_id=1, source_target_pairs={{0,3},{1,0},{2,1},{3,2},{4,7},{5,4},{6,5},{7,6},{8,11},{9,8},{10,9... | collective-permute-start | bytes 491528 | tf_op jit(solution)/shard_map/ppermute | solution.py:430
  68.6 6.9 %second.1 = (f32[320,128]{1,0:T(8,128)S(1)}, f32[320,128]{1,0:T(8,128)S(1)}, f32[320,128]{1,0:T(8,128)S(1)}, f32[320,128]{1,0:T(8,128)S(1)}) custom-call(s32[5]{0:T(128)S(1)} %stack.24.place_ref, f32[160,512]{1,0:T(8,128)S(1)} %collective-permute-done.12.pack_ref, f32[8,80,512]{2,1,0:T(8,128)S(1)} %get-tuple-element.47.y_ref, ...), custom_call_target="tpu_custom_call" | custom-call | flops 3000000000 | bytes 8000000 | tf_op jit(solution)/shard_map/second/pallas_call | solution.py:431
  75.6 0.1 collective-permute-start.16
  75.7 1.8 %collective-permute-start.17 = (f32[320,128]{1,0:T(8,128)S(1)}, f32[320,128]{1,0:T(8,128)S(1)}, u32[]{:S(2)}, u32[]{:S(2)}) collective-permute-start(f32[320,128]{1,0:T(8,128)S(1)} %get-tuple-element.63), channel_id=1, source_target_pairs={{0,2},{1,3},{2,0},{3,1},{4,6},{5,7},{6,4},{7,5},{8,10},{9,11},{10,... | collective-permute-start | bytes 491528 | tf_op jit(solution)/shard_map/ppermute | solution.py:443
  77.4 0.0 collective-permute-done.13.refs_1_
  77.4 0.1 collective-permute-start.18
  77.5 0.0 collective-permute-done.14.refs_2_
  77.5 0.0 collective-permute-done.15.refs_3_
  77.5 3.0 %collective-permute-done.16.refs_5_ = f32[320,128]{1,0:T(8,128)S(1)} collective-permute-done((f32[320,128]{1,0:T(8,128)S(1)}, f32[320,128]{1,0:T(8,128)S(1)}, u32[]{:S(2)}, u32[]{:S(2)}) %collective-permute-start.16) | collective-permute-done | bytes 163872 | tf_op jit(solution)/shard_map/ppermute | solution.py:443
  80.5 1.5 %collective-permute-done.17.refs_6_ = f32[320,128]{1,0:T(8,128)S(1)} collective-permute-done((f32[320,128]{1,0:T(8,128)S(1)}, f32[320,128]{1,0:T(8,128)S(1)}, u32[]{:S(2)}, u32[]{:S(2)}) %collective-permute-start.17) | collective-permute-done | bytes 163872 | tf_op jit(solution)/shard_map/ppermute | solution.py:443
  82.0 4.8 %collective-permute-done.18.refs_7_ = f32[320,128]{1,0:T(8,128)S(1)} collective-permute-done((f32[320,128]{1,0:T(8,128)S(1)}, f32[320,128]{1,0:T(8,128)S(1)}, u32[]{:S(2)}, u32[]{:S(2)}) %collective-permute-start.18) | collective-permute-done | bytes 163872 | tf_op jit(solution)/shard_map/ppermute | solution.py:443
  86.9 1.7 %place.1 = f32[2560,128]{1,0:T(8,128)} custom-call(s32[5]{0:T(128)S(1)} %stack.24.place_ref, f32[320,128]{1,0:T(8,128)S(1)} %get-tuple-element.54.refs_0_, f32[320,128]{1,0:T(8,128)S(1)} %collective-permute-done.13.refs_1_, f32[320,128]{1,0:T(8,128)S(1)} %collective-permute-done.14.refs_2_, f32[320,128]{1,0:T(8,128)S(1)} %collective-permute-done.15.refs_3_, ...), custom_call_target="tpu_custom_call" | custom-call | tf_op jit(solution)/shard_map/place/pallas_call | solution.py:444
  (19 shorter events, 0.1 us)
Async XLA Ops:
  0.0 4.6 %copy-start = (f32[16,20,8,128]{3,2,1,0:T(8,128)S(1)}, f32[16,20,8,128]{3,2,1,0:T(8,128)}, u32[]{:S(2)}) copy-start(f32[16,20,8,128]{3,2,1,0:T(8,128)} %param.6) | copy-start | bytes 3932164
  0.0 4.5 %copy-start.5 = (s32[4,3,256]{2,0,1:T(4,128)S(1)}, s32[4,3,256]{2,0,1:T(4,128)}, u32[]{:S(2)}) copy-start(s32[4,3,256]{2,0,1:T(4,128)} %param.9) | copy-start | bytes 36868
  0.0 23.2 %all-to-all-start = ((f32[16,20,8,128]{3,2,1,0:T(8,128)}), f32[16,20,8,128]{3,2,1,0:T(8,128)S(1)}, u32[]{:S(2)}, u32[]{:S(2)}) async-start(f32[16,20,8,128]{3,2,1,0:T(8,128)} %param.6), calls=%async_computation | async-start | bytes 2621440 | tf_op jit(solution)/shard_map/all_to_all | solution.py:355
  7.5 2.2 %collective-permute-start = (f32[20,512]{1,0:T(8,128)S(1)}, f32[20,512]{1,0:T(8,128)S(1)}, u32[]{:S(2)}, u32[]{:S(2)}) collective-permute-start(f32[20,512]{1,0:T(8,128)S(1)} %get-tuple-element.36), channel_id=1, source_target_pairs={{0,16},{16,0},{1,17},{17,1},{2,18},{18,2},{3,19},{19,3},{4,20},{20... | collective-permute-start | bytes 122888 | tf_op jit(solution)/shard_map/ppermute | solution.py:356
  9.7 8.5 %collective-permute-start.1 = (f32[20,512]{1,0:T(8,128)S(1)}, f32[20,512]{1,0:T(8,128)S(1)}, u32[]{:S(2)}, u32[]{:S(2)}) collective-permute-start(f32[20,512]{1,0:T(8,128)S(1)} %add.22), channel_id=1, source_target_pairs={{0,4},{4,0},{8,12},{12,8},{16,144},{20,148},{24,152},{28,156},{32,... | collective-permute-start | bytes 122888 | tf_op jit(solution)/shard_map/ppermute | solution.py:358
  18.2 34.2 %copy-start.1 = (s32[4,256]{1,0:T(4,128)S(1)}, s32[4,256]{1,0:T(4,128)}, u32[]{:S(2)}) copy-start(s32[4,256]{1,0:T(4,128)} %radius_ref.1) | copy-start | bytes 12292
  18.2 3.9 %collective-permute-start.2 = (f32[20,512]{1,0:T(8,128)S(1)}, f32[20,512]{1,0:T(8,128)S(1)}, u32[]{:S(2)}, u32[]{:S(2)}) collective-permute-start(f32[20,512]{1,0:T(8,128)S(1)} %add.23), channel_id=1, source_target_pairs={{0,8},{4,12},{8,0},{12,4},{16,80},{20,84},{24,88},{28,92},{32,40},... | collective-permute-start | bytes 122888 | tf_op jit(solution)/shard_map/ppermute | solution.py:358
  22.1 5.0 %collective-permute-start.3 = (f32[20,512]{1,0:T(8,128)S(1)}, f32[20,512]{1,0:T(8,128)S(1)}, u32[]{:S(2)}, u32[]{:S(2)}) collective-permute-start(f32[20,512]{1,0:T(8,128)S(1)} %add.24.after_ref), channel_id=1, source_target_pairs={{0,32},{4,36},{8,40},{12,44},{16,48},{20,52},{24,56},{28,60},{32,0... | collective-permute-start | bytes 122888 | tf_op jit(solution)/shard_map/ppermute | solution.py:358
  23.2 31.7 %copy-start.2 = (f32[2,16,8,128]{3,2,1,0:T(8,128)S(1)}, f32[2,16,8,128]{3,2,1,0:T(8,128)}, u32[]{:S(2)}) copy-start(f32[2,16,8,128]{3,2,1,0:T(8,128)} %wind_ref.3) | copy-start | bytes 393220
  23.2 31.7 %copy-start.3 = (f32[4,256]{1,0:T(4,128)S(1)}, f32[4,256]{1,0:T(4,128)}, u32[]{:S(2)}) copy-start(f32[4,256]{1,0:T(4,128)} %value_ref.1) | copy-start | bytes 12292
  23.2 31.7 %copy-start.4 = (f32[4,256]{1,0:T(4,128)S(1)}, f32[4,256]{1,0:T(4,128)}, u32[]{:S(2)}) copy-start(f32[4,256]{1,0:T(4,128)} %error_ref.1) | copy-start | bytes 12292
  24.7 18.7 %collective-permute-start.9 = (f32[80,512]{1,0:T(8,128)S(1)}, f32[80,512]{1,0:T(8,128)S(1)}, u32[]{:S(2)}, u32[]{:S(2)}) collective-permute-start(f32[80,512]{1,0:T(8,128)S(1)} %get-tuple-element.39), channel_id=1, source_target_pairs={{32,16},{64,48},{96,80},{128,112},{160,144},{192,176},{224,208},{1... | collective-permute-start | bytes 491528 | tf_op jit(solution)/shard_map/ppermute | solution.py:374
  27.1 3.0 %collective-permute-start.4 = (f32[20,512]{1,0:T(8,128)S(1)}, f32[20,512]{1,0:T(8,128)S(1)}, u32[]{:S(2)}, u32[]{:S(2)}) collective-permute-start(f32[20,512]{1,0:T(8,128)S(1)} %add.25), channel_id=1, source_target_pairs={{0,64},{4,68},{8,72},{12,76},{16,20},{20,16},{24,28},{28,24},{32,9... | collective-permute-start | bytes 122888 | tf_op jit(solution)/shard_map/ppermute | solution.py:358
  30.1 7.2 %collective-permute-start.5 = (f32[20,512]{1,0:T(8,128)S(1)}, f32[20,512]{1,0:T(8,128)S(1)}, u32[]{:S(2)}, u32[]{:S(2)}) collective-permute-start(f32[20,512]{1,0:T(8,128)S(1)} %add.26), channel_id=1, source_target_pairs={{0,128},{4,132},{8,136},{12,140},{16,24},{20,28},{24,16},{28,20},{... | collective-permute-start | bytes 122888 | tf_op jit(solution)/shard_map/ppermute | solution.py:358
  32.1 8.4 %collective-permute-start.10 = (f32[80,128]{1,0:T(8,128)S(1)}, f32[80,128]{1,0:T(8,128)S(1)}, u32[]{:S(2)}, u32[]{:S(2)}) collective-permute-start(f32[80,128]{1,0:T(8,128)S(1)} %get-tuple-element.40), channel_id=1, source_target_pairs={{0,4},{4,8},{8,12},{1,5},{5,9},{9,13},{2,6},{6,10},{10,14},{3,7},{... | collective-permute-start | bytes 122888 | tf_op jit(solution)/shard_map/ppermute | solution.py:375
  34.0 6.7 %collective-permute-start.11 = (f32[80,128]{1,0:T(8,128)S(1)}, f32[80,128]{1,0:T(8,128)S(1)}, u32[]{:S(2)}, u32[]{:S(2)}) collective-permute-start(f32[80,128]{1,0:T(8,128)S(1)} %get-tuple-element.41), channel_id=1, source_target_pairs={{4,0},{8,4},{12,8},{5,1},{9,5},{13,9},{6,2},{10,6},{14,10},{7,3},{... | collective-permute-start | bytes 122888 | tf_op jit(solution)/shard_map/ppermute | solution.py:376
  37.4 3.3 %collective-permute-start.8 = (f32[20,512]{1,0:T(8,128)S(1)}, f32[20,512]{1,0:T(8,128)S(1)}, u32[]{:S(2)}, u32[]{:S(2)}) collective-permute-start(f32[20,512]{1,0:T(8,128)S(1)} %add.27.own_ref), channel_id=1, source_target_pairs={{0,1},{1,2},{2,3},{3,0},{4,5},{5,6},{6,7},{7,4},{8,9},{9,10},{10,1... | collective-permute-start | bytes 122888 | tf_op jit(solution)/shard_map/ppermute | solution.py:382
  38.0 4.4 %collective-permute-start.7 = (f32[20,512]{1,0:T(8,128)S(1)}, f32[20,512]{1,0:T(8,128)S(1)}, u32[]{:S(2)}, u32[]{:S(2)}) collective-permute-start(f32[20,512]{1,0:T(8,128)S(1)} %add.27.own_ref), channel_id=1, source_target_pairs={{0,2},{1,3},{2,0},{3,1},{4,6},{5,7},{6,4},{7,5},{8,10},{9,11},{10,... | collective-permute-start | bytes 122888 | tf_op jit(solution)/shard_map/ppermute | solution.py:382
  40.4 2.9 %collective-permute-start.6 = (f32[20,512]{1,0:T(8,128)S(1)}, f32[20,512]{1,0:T(8,128)S(1)}, u32[]{:S(2)}, u32[]{:S(2)}) collective-permute-start(f32[20,512]{1,0:T(8,128)S(1)} %add.27.own_ref), channel_id=1, source_target_pairs={{0,3},{1,0},{2,1},{3,2},{4,7},{5,4},{6,5},{7,6},{8,11},{9,8},{10,9... | collective-permute-start | bytes 122888 | tf_op jit(solution)/shard_map/ppermute | solution.py:382
  43.4 11.5 %collective-permute-start.12 = (f32[160,512]{1,0:T(8,128)S(1)}, f32[160,512]{1,0:T(8,128)S(1)}, u32[]{:S(2)}, u32[]{:S(2)}) collective-permute-start(f32[160,512]{1,0:T(8,128)S(1)} %stack.25.after_ref), channel_id=1, source_target_pairs={{0,16},{16,0},{1,17},{17,1},{2,18},{18,2},{3,19},{19,3},{4,20},{20... | collective-permute-start | bytes 983048 | tf_op jit(solution)/shard_map/ppermute | solution.py:392
  64.0 13.4 %collective-permute-start.13 = (f32[320,128]{1,0:T(8,128)S(1)}, f32[320,128]{1,0:T(8,128)S(1)}, u32[]{:S(2)}, u32[]{:S(2)}) collective-permute-start(f32[320,128]{1,0:T(8,128)S(1)} %get-tuple-element.55), channel_id=1, source_target_pairs={{0,1},{1,2},{2,3},{3,0},{4,5},{5,6},{6,7},{7,4},{8,9},{9,10},{10,1... | collective-permute-start | bytes 491528 | tf_op jit(solution)/shard_map/ppermute | solution.py:430
  64.8 12.7 %collective-permute-start.14 = (f32[320,128]{1,0:T(8,128)S(1)}, f32[320,128]{1,0:T(8,128)S(1)}, u32[]{:S(2)}, u32[]{:S(2)}) collective-permute-start(f32[320,128]{1,0:T(8,128)S(1)} %get-tuple-element.56), channel_id=1, source_target_pairs={{0,2},{1,3},{2,0},{3,1},{4,6},{5,7},{6,4},{7,5},{8,10},{9,11},{10,... | collective-permute-start | bytes 491528 | tf_op jit(solution)/shard_map/ppermute | solution.py:430
  67.1 10.4 %collective-permute-start.15 = (f32[320,128]{1,0:T(8,128)S(1)}, f32[320,128]{1,0:T(8,128)S(1)}, u32[]{:S(2)}, u32[]{:S(2)}) collective-permute-start(f32[320,128]{1,0:T(8,128)S(1)} %get-tuple-element.57), channel_id=1, source_target_pairs={{0,3},{1,0},{2,1},{3,2},{4,7},{5,4},{6,5},{7,6},{8,11},{9,8},{10,9... | collective-permute-start | bytes 491528 | tf_op jit(solution)/shard_map/ppermute | solution.py:430
  75.6 5.0 %collective-permute-start.16 = (f32[320,128]{1,0:T(8,128)S(1)}, f32[320,128]{1,0:T(8,128)S(1)}, u32[]{:S(2)}, u32[]{:S(2)}) collective-permute-start(f32[320,128]{1,0:T(8,128)S(1)} %get-tuple-element.62), channel_id=1, source_target_pairs={{0,1},{1,2},{2,3},{3,0},{4,5},{5,6},{6,7},{7,4},{8,9},{9,10},{10,1... | collective-permute-start | bytes 491528 | tf_op jit(solution)/shard_map/ppermute | solution.py:443
  75.7 6.4 %collective-permute-start.17 = (f32[320,128]{1,0:T(8,128)S(1)}, f32[320,128]{1,0:T(8,128)S(1)}, u32[]{:S(2)}, u32[]{:S(2)}) collective-permute-start(f32[320,128]{1,0:T(8,128)S(1)} %get-tuple-element.63), channel_id=1, source_target_pairs={{0,2},{1,3},{2,0},{3,1},{4,6},{5,7},{6,4},{7,5},{8,10},{9,11},{10,... | collective-permute-start | bytes 491528 | tf_op jit(solution)/shard_map/ppermute | solution.py:443
  77.4 9.4 %collective-permute-start.18 = (f32[320,128]{1,0:T(8,128)S(1)}, f32[320,128]{1,0:T(8,128)S(1)}, u32[]{:S(2)}, u32[]{:S(2)}) collective-permute-start(f32[320,128]{1,0:T(8,128)S(1)} %get-tuple-element.64), channel_id=1, source_target_pairs={{0,3},{1,0},{2,1},{3,2},{4,7},{5,4},{6,5},{7,6},{8,11},{9,8},{10,9... | collective-permute-start | bytes 491528 | tf_op jit(solution)/shard_map/ppermute | solution.py:443

commit v2 on v1

--- a/solution.py
+++ b/solution.py
@@ -1,3 +1,5 @@
+import functools
+
 import jax
 import jax.numpy as jnp
 from jax import lax
@@ -22,40 +24,41 @@
     return high, (x - high.astype(F32)).astype(BF16)
 
 
-def pick_kernel(place_ref, where_ref, state_ref, keep_ref, give_ref, parts_ref, found_ref):
+def pick_kernel(
+    place_ref, where_ref, state_ref, keep_ref, give_ref, cut0_ref, cut1_ref, cut2_ref, cut3_ref, parts_ref, found_ref
+):
     row_start, col_start, core = place_ref[0], place_ref[1], place_ref[2]
     cells = state_ref.shape[0] // 8
     levels = found_ref.shape[0] // keep_ref.shape[0]
     members = keep_ref.shape[0]
     cols = state_ref.shape[1]
     n_obs = where_ref.shape[2]
-    halves = where_ref.shape[0] // 2
+    halves = where_ref.shape[1] // 2
     for row in range(8):
         x = state_ref[pl.ds(row, cells, stride=8), :]
-        high = x.astype(BF16)
-        rest = x - high.astype(F32)
-        mid = rest.astype(BF16)
-        low = (rest - mid.astype(F32)).astype(BF16)
-        for at, part in enumerate((high, mid, low)):
+        for at, part in enumerate(split(x)):
             parts_ref[at * cells : (at + 1) * cells, row * cols : (row + 1) * cols] = part
     cell = lax.broadcasted_iota(jnp.int32, (8 * cols, n_obs), 0)
     for half, out_ref in enumerate((keep_ref, give_ref)):
         for at in range(halves):
             batch = lax.rem(core + half, 2) * halves + at
-            places = where_ref[batch]
-            lev = places[0:1, :]
-            row = places[1:2, :] - row_start
-            col = places[2:3, :] - col_start
+            lev, row, col = (where_ref[k, pl.ds(batch, 1), :] for k in range(3))
+            row = row - row_start
+            col = col - col_start
             owned = (row >= 0) & (row < 8) & (col >= 0) & (col < cols)
             key = jnp.where(owned, row * cols + col, -1)
             hot = jnp.where(cell == key, 1.0, 0.0).astype(BF16)
             got = jnp.dot(parts_ref[...], hot, preferred_element_type=F32)
-            found_ref[...] = got[:cells] + got[cells : 2 * cells] + got[2 * cells :]
+            found_ref[...] = got[:cells] + got[cells:]
             total = jnp.zeros((members, n_obs), F32)
             for level in range(levels):
                 rows = found_ref[level * members : (level + 1) * members, :]
                 total = total + jnp.where(lev == level, rows, 0.0)
             out_ref[:, at * n_obs : (at + 1) * n_obs] = total
+    length = cut0_ref.shape[0]
+    for share, ref in enumerate((cut0_ref, cut1_ref, cut2_ref, cut3_ref)):
+        target = lax.rem(place_ref[3] + share, 4)
+        ref[...] = state_ref[pl.ds(pl.multiple_of(target * length, length), length), :]
 
 
 def stack_kernel(own_ref, one_ref, two_ref, three_ref, inner_ref, out_ref):
@@ -78,18 +81,15 @@
     return jnp.concatenate([block] * (lanes // 128), axis=1)
 
 
-def lay_kernel(place_ref, cur_ref, after_ref, y_ref, far_ref, near_ref, left_ref, right_ref):
-    me = place_ref[3]
-    cols = cur_ref.shape[1]
+def lay_kernel(place_ref, own_ref, one_ref, two_ref, three_ref, after_ref, y_ref, far_ref, near_ref, left_ref, right_ref):
+    cols = own_ref.shape[1]
     shares = 4
     levels = y_ref.shape[2] // cols
     members = y_ref.shape[1] // shares
-    for share in range(shares):
-        source = lax.rem(me + share, shares)
+    for share, cur_ref in enumerate((own_ref, one_ref, two_ref, three_ref)):
         for level in range(levels):
-            base = (source * levels + level) * members * 8
             for row in range(8):
-                got = cur_ref[pl.ds(base + row, members, stride=8), :]
+                got = cur_ref[pl.ds(level * members * 8 + row, members, stride=8), :]
                 y_ref[row, share * members : (share + 1) * members, level * cols : (level + 1) * cols] = got
     core = place_ref[2]
     far_ref[...] = y_ref[7 * core]
@@ -107,13 +107,13 @@
     right_ref[...] = right
 
 
-def taper_kernel(place_ref, where_ref, radius_ref, after_ref, w_ref, wc_ref, wo_ref):
+def row_taper_kernel(place_ref, where_ref, radius_ref, after_ref, w_ref):
     row_start, col_start = place_ref[0], place_ref[1]
-    batches, _, n_obs = where_ref.shape
+    _, batches, n_obs = where_ref.shape
     cols = w_ref.shape[2]
     lane_w = lax.broadcasted_iota(jnp.int32, (n_obs, cols), 1)
     for batch in range(batches):
-        places = where_ref[batch].astype(F32)
+        places = where_ref[:, batch, :].astype(F32)
         q = radius_ref[batch : batch + 1, :].astype(F32)
         obs_row, obs_col = down(places[1:2, :]), down(places[2:3, :])
         reach = down(1.0 / (4.0 * q * q))
@@ -122,11 +122,23 @@
         for row in range(10):
             off = (row_start + (row - 1)).astype(F32) - obs_row
             w_ref[batch * 10 + row] = taper(off * off + gap, reach)
+
+
+def taper_kernel(place_ref, where_ref, radius_ref, after_ref, wc_ref, wo_ref):
+    row_start, col_start = place_ref[0], place_ref[1]
+    _, batches, n_obs = where_ref.shape
+    cols = wc_ref.shape[2]
+    lane_w = lax.broadcasted_iota(jnp.int32, (n_obs, cols), 1)
+    for batch in range(batches):
+        places = where_ref[:, batch, :].astype(F32)
+        q = radius_ref[batch : batch + 1, :].astype(F32)
+        obs_row, obs_col = down(places[1:2, :]), down(places[2:3, :])
+        reach = down(1.0 / (4.0 * q * q))
         edge_row = (row_start + lane_w % 8).astype(F32) - obs_row
         edge_col = jnp.where(lane_w < 32, col_start - 1, col_start + cols).astype(F32) - obs_col
         wc_ref[batch] = taper(edge_row * edge_row + edge_col * edge_col, reach)
         for later in range(batch + 1, batches):
-            others = where_ref[later].astype(F32)
+            others = where_ref[:, later, :].astype(F32)
             off = others[1:2, :] - wide(obs_row, n_obs)
             gap_o = others[2:3, :] - wide(obs_col, n_obs)
             pair = batch * (2 * batches - batch - 1) // 2 + later - batch - 1
@@ -275,14 +287,14 @@
     transported(first, place_ref, z_ref, edge_ref, wind_ref, f_ref, (out0_ref, out1_ref, out2_ref, out3_ref))
 
 
-def place_kernel(place_ref, *refs):
-    blocks, out_ref, sems = refs[:8], refs[8], refs[9]
+def place_kernel(spots, place_ref, *refs):
+    blocks, out_ref, sems = refs[: len(spots)], refs[-2], refs[-1]
     me = place_ref[3]
     length = blocks[0].shape[0]
     copies = []
-    for at, block in enumerate(blocks):
-        source = lax.rem(me + 4 - at % 4, 4)
-        start = pl.multiple_of((source * 2 + at // 4) * length, length)
+    for at, ((back, half), block) in enumerate(zip(spots, blocks)):
+        source = lax.rem(me + 4 - back, 4)
+        start = pl.multiple_of((source * 2 + half) * length, length)
         copies.append(pltpu.make_async_copy(block, out_ref.at[pl.ds(start, length)], sems.at[at]))
     for copy in copies:
         copy.start()
@@ -323,7 +335,7 @@
                     axis, bit = orders[core % 2][at]
                     to_z, to_x = (z ^ bit, x) if axis == "z" else (z, x ^ bit)
                     pairs.append(((z * cores + core) * across + x, (to_z * cores + core) * across + to_x))
-        steps.append(pairs)
+        steps.append([pairs])
     return steps
 
 
@@ -339,24 +351,29 @@
         [lax.axis_index(GX) * tile_rows, lax.axis_index("gy") * tile_cols, lax.axis_index("gx_1"), me, me * here]
     ).astype(jnp.int32)
     flat = levels * share_size * tile_rows
+    obs_where = jnp.swapaxes(obs_where, 0, 1)
     vmem = pl.BlockSpec(memory_space=VMEM)
     smem = pl.BlockSpec(memory_space=SMEM)
     cells = levels * share_size
-    keep, give = pl.pallas_call(
+    keep, give, *cuts = pl.pallas_call(
         pick_kernel,
-        out_shape=[jax.ShapeDtypeStruct((share_size, half), F32)] * 2,
+        out_shape=[jax.ShapeDtypeStruct((share_size, half), F32)] * 2
+        + [jax.ShapeDtypeStruct((flat // shares, tile_cols), F32)] * shares,
         in_specs=[smem, vmem, vmem],
-        out_specs=[vmem, vmem],
-        scratch_shapes=[VMEM((3 * cells, tile_rows * tile_cols), BF16), VMEM((cells, n_obs), F32)],
+        out_specs=[vmem] * 6,
+        scratch_shapes=[VMEM((2 * cells, tile_rows * tile_cols), BF16), VMEM((cells, n_obs), F32)],
         compiler_params=pltpu.CompilerParams(vmem_limit_bytes=16 << 20),
         name="pick",
     )(place, obs_where, state.reshape(flat, tile_cols))
     any_ = pl.BlockSpec(memory_space=pl.ANY)
-    cur = lax.all_to_all(state, "ens", split_axis=0, concat_axis=0, tiled=True)
     x = keep + lax.ppermute(give, "gx_1", ring("gx_1", 1))
-    for step, pairs in enumerate(exchanges(), start=1):
-        got = lax.ppermute(x, (*GX, "gy"), pairs)
-        if step == 3:
+    for step, permutations in enumerate(exchanges(), start=1):
+        got = [lax.ppermute(x, (*GX, "gy"), pairs) for pairs in permutations]
+        if step == 1:
+            came = []
+            for k in (3, 2, 1):
+                came.append(lax.ppermute(cuts[k], "ens", ring("ens", k)))
+        if step == 4:
             line_shape = jax.ShapeDtypeStruct((members, here * tile_cols), F32)
             edge_shape = jax.ShapeDtypeStruct((members, tile_cols), F32)
             y, outer, inner, left, right = pl.pallas_call(
@@ -365,21 +382,30 @@
                     jax.ShapeDtypeStruct((tile_rows, members, here * tile_cols), F32),
                     line_shape, line_shape, edge_shape, edge_shape,
                 ],
-                in_specs=[smem, vmem, any_],
+                in_specs=[smem, vmem, vmem, vmem, vmem, any_],
                 out_specs=[vmem] * 5,
                 compiler_params=pltpu.CompilerParams(vmem_limit_bytes=12 << 20),
                 cost_estimate=pl.CostEstimate(flops=2_000_000, bytes_accessed=4_000_000, transcendentals=0),
                 name="lay",
-            )(place, cur.reshape(flat, tile_cols), x)
+            )(place, cuts[0], *came, x)
             far = lax.ppermute(outer, GX, beyond())
             from_left = lax.ppermute(right, "gy", line("gy", 1))
             from_right = lax.ppermute(left, "gy", line("gy", -1))
-            got, y = lax.optimization_barrier((got, y))
-        x = x + got
+            *got, y = lax.optimization_barrier((*got, y))
+        x = x + sum(got[1:], got[0])
     own = x
     gathered = [own]
     for k in (1, 2, 3):
         gathered.append(lax.ppermute(own, "ens", ring("ens", -k)))
+    w = pl.pallas_call(
+        row_taper_kernel,
+        out_shape=jax.ShapeDtypeStruct((batches * 10, n_obs, tile_cols), F32),
+        in_specs=[smem, vmem, vmem, any_],
+        out_specs=vmem,
+        compiler_params=pltpu.CompilerParams(vmem_limit_bytes=12 << 20),
+        cost_estimate=pl.CostEstimate(flops=15_000_000, bytes_accessed=6_000_000, transcendentals=0),
+        name="row_taper",
+    )(place, obs_where, radius, own)
     own, one, two, three, far, from_left, from_right = lax.optimization_barrier((*gathered, far, from_left, from_right))
     stacked = pl.pallas_call(
         stack_kernel,
@@ -391,17 +417,16 @@
     )(own, one, two, three, inner)
     pack = lax.ppermute(stacked, "gx_1", ring("gx_1", 1))
     pairs = batches * (batches - 1) // 2
-    w, wc, wo = pl.pallas_call(
+    wc, wo = pl.pallas_call(
         taper_kernel,
         out_shape=[
-            jax.ShapeDtypeStruct((batches * 10, n_obs, tile_cols), F32),
             jax.ShapeDtypeStruct((batches, n_obs, tile_cols), F32),
             jax.ShapeDtypeStruct((pairs, n_obs, n_obs), F32),
         ],
         in_specs=[smem, vmem, vmem, any_],
-        out_specs=[vmem] * 3,
-        compiler_params=pltpu.CompilerParams(vmem_limit_bytes=20 << 20),
-        cost_estimate=pl.CostEstimate(flops=20_000_000, bytes_accessed=8_000_000, transcendentals=0),
+        out_specs=[vmem] * 2,
+        compiler_params=pltpu.CompilerParams(vmem_limit_bytes=8 << 20),
+        cost_estimate=pl.CostEstimate(flops=5_000_000, bytes_accessed=2_000_000, transcendentals=0),
         name="taper",
     )(place, obs_where, radius, stacked)
     width = here // 2 * tile_cols
@@ -425,7 +450,7 @@
         place, obs_value, obs_error, own, one, two, three, pack,
         y, far, from_left, from_right, w, wc, wo, wind,
     )
-    back = [early[0]]
+    back = []
     for k in (1, 2, 3):
         back.append(lax.ppermute(early[k], "ens", ring("ens", k)))
     late = pl.pallas_call(
@@ -438,18 +463,25 @@
         cost_estimate=pl.CostEstimate(flops=3_000_000_000, bytes_accessed=8_000_000, transcendentals=0),
         name="second",
     )(place, pack, y, far, s3, n2, edge, w, wind)
-    back.append(late[0])
+    last = []
     for k in (1, 2, 3):
-        back.append(lax.ppermute(late[k], "ens", ring("ens", k)))
-    out = pl.pallas_call(
-        place_kernel,
-        out_shape=jax.ShapeDtypeStruct((flat, tile_cols), F32),
-        in_specs=[smem] + [vmem] * 8,
-        out_specs=any_,
-        scratch_shapes=[pltpu.SemaphoreType.DMA((8,))],
-        compiler_params=pltpu.CompilerParams(vmem_limit_bytes=8 << 20),
-        name="place",
-    )(place, *back)
+        last.append(lax.ppermute(late[k], "ens", ring("ens", k)))
+
+    def placed(blocks, spots, out):
+        more = [] if out is None else [out]
+        return pl.pallas_call(
+            functools.partial(place_kernel, spots),
+            out_shape=jax.ShapeDtypeStruct((flat, tile_cols), F32),
+            in_specs=[smem] + [vmem] * len(blocks) + [any_] * len(more),
+            out_specs=any_,
+            scratch_shapes=[pltpu.SemaphoreType.DMA((len(blocks),))],
+            input_output_aliases={1 + len(blocks): 0} if more else {},
+            compiler_params=pltpu.CompilerParams(vmem_limit_bytes=4 << 20),
+            name="place",
+        )(place, *blocks, *more)
+
+    out = placed([early[0], *back, late[0]], ((0, 0), (1, 0), (2, 0), (3, 0), (0, 1)), None)
+    out = placed(last, ((1, 1), (2, 1), (3, 1)), out)
     return out.reshape(levels, share_size, tile_rows, tile_cols)
 
 

time: 88.9 us -> 92.2 us (1.037)
  the two profiles are of different devices: /device:TPU:11 before, /device:TPU:1 now
where the time goes in v2:
time: 92.2 us; the launch traced here: 90.5 us
  starting transfers between devices  46 us (50%)
  Pallas kernels  25.9 us (28%)
  waiting for transfers between devices  16.1 us (17%)
  local copies, waits for them, and re-layouts  2.13 us (2%)
    ppermute x5, starting transfers between devices, shards(): got = [lax.ppermute(x, (*GX, 'gy'), pairs) for pairs in permutations]  13.5 us
    ppermute x1, starting transfers between devices, shards(): pack = lax.ppermute(stacked, 'gx_1', ring('gx_1', 1))  9.29 us
    pallas_call x1, Pallas kernels, shards(): pl.pallas_call(first_kernel, out_shape=[piece, piece, piece, piece, jax.S...  9.07 us
    ppermute x5, waiting for transfers between devices, shards(): got = [lax.ppermute(x, (*GX, 'gy'), pairs) for pairs in permutations]  8.12 us
    pallas_call x1, Pallas kernels, shards(): pl.pallas_call(second_kernel, out_shape=[piece] * 4, in_specs=[smem] + [v...  6.93 us
    ppermute x3, waiting for transfers between devices, shards(): last.append(lax.ppermute(late[k], 'ens', ring('ens', k)))  5.05 us
    ppermute x3, starting transfers between devices, shards(): came.append(lax.ppermute(cuts[k], 'ens', ring('ens', k)))  4.67 us
    ppermute x3, starting transfers between devices, shards(): last.append(lax.ppermute(late[k], 'ens', ring('ens', k)))  3.71 us
  transfers between devices with their start and end apart: 22, of which 12 were waited for; matrix products, arithmetic and copies ran while one was open for 0% of the time, Pallas kernels for 13%

profile of v2, /device:TPU:1, one launch (start us, length us, event | category | flops | bytes accessed | tf_op | source)
XLA Modules:
  0.0 90.5 jit_solution(70520268997047450)
XLA Ops:
  0.0 0.1 stack.24.place_ref
  0.1 1.3 %copy-done = f32[16,20,8,128]{3,2,1,0:T(8,128)S(1)} copy-done((f32[16,20,8,128]{3,2,1,0:T(8,128)S(1)}, f32[16,20,8,128]{3,2,1,0:T(8,128)}, u32[]{:S(2)}) %copy-start) | copy-done | bytes 1310744
  1.4 0.7 copy-done.1
  2.1 2.3 %pick.1 = (f32[20,512]{1,0:T(8,128)S(1)}, f32[20,512]{1,0:T(8,128)S(1)}, f32[640,128]{1,0:T(8,128)S(1)}, f32[640,128]{1,0:T(8,128)S(1)}, f32[640,128]{1,0:T(8,128)S(1)}, /*index=5*/f32[640,128]{1,0:T(8,128)S(1)}) custom-call(s32[5]{0:T(128)S(1)} %stack.24.place_ref, s32[3,4,256]{2,1,0:T(4,128)S(1)} %bitcast.9, f32[2560,128]{1,0:T(8,128)S(1)} %bitcast.8), custom_call_target="tpu_custom_call" | custom-call | tf_op jit(solution)/shard_map/pick/pallas_call | solution.py:358
  4.4 3.6 %collective-permute-start.5 = (f32[640,128]{1,0:T(8,128)S(1)}, f32[640,128]{1,0:T(8,128)S(1)}, u32[]{:S(2)}, u32[]{:S(2)}) collective-permute-start(f32[640,128]{1,0:T(8,128)S(1)} %get-tuple-element.41), channel_id=1, source_target_pairs={{0,3},{1,0},{2,1},{3,2},{4,7},{5,4},{6,5},{7,6},{8,11},{9,8},{10,9... | collective-permute-start | bytes 983048 | tf_op jit(solution)/shard_map/ppermute | solution.py:375
  8.1 0.3 collective-permute-start.6
  8.4 0.7 collective-permute-start.7
  9.1 1.5 %collective-permute-start = (f32[20,512]{1,0:T(8,128)S(1)}, f32[20,512]{1,0:T(8,128)S(1)}, u32[]{:S(2)}, u32[]{:S(2)}) collective-permute-start(f32[20,512]{1,0:T(8,128)S(1)} %get-tuple-element.39), channel_id=1, source_target_pairs={{0,16},{16,0},{1,17},{17,1},{2,18},{18,2},{3,19},{19,3},{4,20},{20... | collective-permute-start | bytes 122888 | tf_op jit(solution)/shard_map/ppermute | solution.py:369
  10.6 0.9 collective-permute-done
  11.5 7.0 %collective-permute-start.1 = (f32[20,512]{1,0:T(8,128)S(1)}, f32[20,512]{1,0:T(8,128)S(1)}, u32[]{:S(2)}, u32[]{:S(2)}) collective-permute-start(f32[20,512]{1,0:T(8,128)S(1)} %add.22), channel_id=1, source_target_pairs={{0,4},{4,0},{8,12},{12,8},{16,144},{20,148},{24,152},{28,156},{32,... | collective-permute-start | bytes 122888 | tf_op jit(solution)/shard_map/ppermute | solution.py:371
  18.5 1.5 %collective-permute-done.1 = f32[20,512]{1,0:T(8,128)S(1)} collective-permute-done((f32[20,512]{1,0:T(8,128)S(1)}, f32[20,512]{1,0:T(8,128)S(1)}, u32[]{:S(2)}, u32[]{:S(2)}) %collective-permute-start.1) | collective-permute-done | bytes 40992 | tf_op jit(solution)/shard_map/ppermute | solution.py:371
  20.0 0.0 copy-start.2
  20.0 1.5 %collective-permute-start.2 = (f32[20,512]{1,0:T(8,128)S(1)}, f32[20,512]{1,0:T(8,128)S(1)}, u32[]{:S(2)}, u32[]{:S(2)}) collective-permute-start(f32[20,512]{1,0:T(8,128)S(1)} %add.23), channel_id=1, source_target_pairs={{0,8},{4,12},{8,0},{12,4},{16,80},{20,84},{24,88},{28,92},{32,40},... | collective-permute-start | bytes 122888 | tf_op jit(solution)/shard_map/ppermute | solution.py:371
  21.5 2.7 %collective-permute-done.2 = f32[20,512]{1,0:T(8,128)S(1)} collective-permute-done((f32[20,512]{1,0:T(8,128)S(1)}, f32[20,512]{1,0:T(8,128)S(1)}, u32[]{:S(2)}, u32[]{:S(2)}) %collective-permute-start.2) | collective-permute-done | bytes 40992 | tf_op jit(solution)/shard_map/ppermute | solution.py:371
  24.2 0.8 collective-permute-start.3
  25.1 2.2 %collective-permute-done.3 = f32[20,512]{1,0:T(8,128)S(1)} collective-permute-done((f32[20,512]{1,0:T(8,128)S(1)}, f32[20,512]{1,0:T(8,128)S(1)}, u32[]{:S(2)}, u32[]{:S(2)}) %collective-permute-start.3) | collective-permute-done | bytes 40992 | tf_op jit(solution)/shard_map/ppermute | solution.py:371
  27.3 1.4 %lay.1 = (f32[8,80,512]{2,1,0:T(8,128)S(1)}, f32[80,512]{1,0:T(8,128)S(1)}, f32[80,512]{1,0:T(8,128)S(1)}, f32[80,128]{1,0:T(8,128)S(1)}, f32[80,128]{1,0:T(8,128)S(1)}) custom-call(s32[5]{0:T(128)S(1)} %stack.24.place_ref, f32[640,128]{1,0:T(8,128)S(1)} %get-tuple-element.40.own_ref, f32[640,128]{1,0:T(8,128)S(1)} %collective-permute-done.5.one_ref, ...), custom_call_target="tpu_custom_call" | custom-call | flops 2000000 | bytes 4000000 | tf_op jit(solution)/shard_map/lay/pallas_call | solution.py:379
  28.8 2.8 %collective-permute-start.12 = (f32[80,512]{1,0:T(8,128)S(1)}, f32[80,512]{1,0:T(8,128)S(1)}, u32[]{:S(2)}, u32[]{:S(2)}) collective-permute-start(f32[80,512]{1,0:T(8,128)S(1)} %get-tuple-element.46), channel_id=1, source_target_pairs={{32,16},{64,48},{96,80},{128,112},{160,144},{192,176},{224,208},{1... | collective-permute-start | bytes 491528 | tf_op jit(solution)/shard_map/ppermute | solution.py:391
  31.6 1.3 %collective-permute-start.4 = (f32[20,512]{1,0:T(8,128)S(1)}, f32[20,512]{1,0:T(8,128)S(1)}, u32[]{:S(2)}, u32[]{:S(2)}) collective-permute-start(f32[20,512]{1,0:T(8,128)S(1)} %add.25.after_ref), channel_id=1, source_target_pairs={{0,64},{4,68},{8,72},{12,76},{16,20},{20,16},{24,28},{28,24},{32,9... | collective-permute-start | bytes 122888 | tf_op jit(solution)/shard_map/ppermute | solution.py:371
  32.9 1.7 %collective-permute-done.4 = f32[20,512]{1,0:T(8,128)S(1)} collective-permute-done((f32[20,512]{1,0:T(8,128)S(1)}, f32[20,512]{1,0:T(8,128)S(1)}, u32[]{:S(2)}, u32[]{:S(2)}) %collective-permute-start.4) | collective-permute-done | bytes 40992 | tf_op jit(solution)/shard_map/ppermute | solution.py:371
  34.6 2.8 %collective-permute-start.8 = (f32[20,512]{1,0:T(8,128)S(1)}, f32[20,512]{1,0:T(8,128)S(1)}, u32[]{:S(2)}, u32[]{:S(2)}) collective-permute-start(f32[20,512]{1,0:T(8,128)S(1)} %add.26), channel_id=1, source_target_pairs={{0,128},{4,132},{8,136},{12,140},{16,24},{20,28},{24,16},{28,20},{... | collective-permute-start | bytes 122888 | tf_op jit(solution)/shard_map/ppermute | solution.py:371
  37.5 2.2 %collective-permute-start.13 = (f32[80,128]{1,0:T(8,128)S(1)}, f32[80,128]{1,0:T(8,128)S(1)}, u32[]{:S(2)}, u32[]{:S(2)}) collective-permute-start(f32[80,128]{1,0:T(8,128)S(1)} %get-tuple-element.47), channel_id=1, source_target_pairs={{0,4},{4,8},{8,12},{1,5},{5,9},{9,13},{2,6},{6,10},{10,14},{3,7},{... | collective-permute-start | bytes 122888 | tf_op jit(solution)/shard_map/ppermute | solution.py:392
  39.7 1.3 %collective-permute-start.14 = (f32[80,128]{1,0:T(8,128)S(1)}, f32[80,128]{1,0:T(8,128)S(1)}, u32[]{:S(2)}, u32[]{:S(2)}) collective-permute-start(f32[80,128]{1,0:T(8,128)S(1)} %get-tuple-element.48), channel_id=1, source_target_pairs={{4,0},{8,4},{12,8},{5,1},{9,5},{13,9},{6,2},{10,6},{14,10},{7,3},{... | collective-permute-start | bytes 122888 | tf_op jit(solution)/shard_map/ppermute | solution.py:393
  41.0 0.9 %collective-permute-start.11 = (f32[20,512]{1,0:T(8,128)S(1)}, f32[20,512]{1,0:T(8,128)S(1)}, u32[]{:S(2)}, u32[]{:S(2)}) collective-permute-start(f32[20,512]{1,0:T(8,128)S(1)} %add.27.own_ref.after_ref), channel_id=1, source_target_pairs={{0,1},{1,2},{2,3},{3,0},{4,5},{5,6},{6,7},{7,4},{8,9},{9,10},{10,1... | collective-permute-start | bytes 122888 | tf_op jit(solution)/shard_map/ppermute | solution.py:399
  42.0 1.6 %collective-permute-start.10 = (f32[20,512]{1,0:T(8,128)S(1)}, f32[20,512]{1,0:T(8,128)S(1)}, u32[]{:S(2)}, u32[]{:S(2)}) collective-permute-start(f32[20,512]{1,0:T(8,128)S(1)} %add.27.own_ref.after_ref), channel_id=1, source_target_pairs={{0,2},{1,3},{2,0},{3,1},{4,6},{5,7},{6,4},{7,5},{8,10},{9,11},{10,... | collective-permute-start | bytes 122888 | tf_op jit(solution)/shard_map/ppermute | solution.py:399
  43.5 0.9 %collective-permute-start.9 = (f32[20,512]{1,0:T(8,128)S(1)}, f32[20,512]{1,0:T(8,128)S(1)}, u32[]{:S(2)}, u32[]{:S(2)}) collective-permute-start(f32[20,512]{1,0:T(8,128)S(1)} %add.27.own_ref.after_ref), channel_id=1, source_target_pairs={{0,3},{1,0},{2,1},{3,2},{4,7},{5,4},{6,5},{7,6},{8,11},{9,8},{10,9... | collective-permute-start | bytes 122888 | tf_op jit(solution)/shard_map/ppermute | solution.py:399
  44.5 0.3 collective-permute-done.14.right_ref
  44.7 0.5 collective-permute-done.11.three_ref
  45.2 1.2 %collective-permute-done.10.two_ref = f32[20,512]{1,0:T(8,128)S(1)} collective-permute-done((f32[20,512]{1,0:T(8,128)S(1)}, f32[20,512]{1,0:T(8,128)S(1)}, u32[]{:S(2)}, u32[]{:S(2)}) %collective-permute-start.10) | collective-permute-done | bytes 40992 | tf_op jit(solution)/shard_map/ppermute | solution.py:399
  46.4 0.1 collective-permute-done.9.one_ref
  46.5 0.0 copy-start.3
  46.5 0.0 copy-start.5
  46.5 9.3 %collective-permute-start.15 = (f32[160,512]{1,0:T(8,128)S(1)}, f32[160,512]{1,0:T(8,128)S(1)}, u32[]{:S(2)}, u32[]{:S(2)}) collective-permute-start(f32[160,512]{1,0:T(8,128)S(1)} %stack.25.after_ref), channel_id=1, source_target_pairs={{0,16},{16,0},{1,17},{17,1},{2,18},{18,2},{3,19},{19,3},{4,20},{20... | collective-permute-start | bytes 983048 | tf_op jit(solution)/shard_map/ppermute | solution.py:418
  55.8 2.0 %row_taper.1.w_ref = f32[40,256,128]{2,1,0:T(8,128)S(1)} custom-call(s32[5]{0:T(128)S(1)} %stack.24.place_ref, s32[3,4,256]{2,1,0:T(4,128)S(1)} %bitcast.10, s32[4,256]{1,0:T(4,128)S(1)} %copy-done.2, f32[20,512]{1,0:T(8,128)S(1)} %add.27.own_ref.after_ref), custom_call_target="tpu_custom_call" | custom-call | flops 15000000 | bytes 6000000 | tf_op jit(solution)/shard_map/row_taper/pallas_call | solution.py:400
  57.8 1.3 %taper.1 = (f32[4,256,128]{2,1,0:T(8,128)S(1)}, f32[6,256,256]{2,1,0:T(8,128)S(1)}) custom-call(s32[5]{0:T(128)S(1)} %stack.24.place_ref, s32[3,4,256]{2,1,0:T(4,128)S(1)} %bitcast.11, s32[4,256]{1,0:T(4,128)S(1)} %copy-done.2, f32[160,512]{1,0:T(8,128)S(1)} %stack.25.after_ref), custom_call_target="tpu_custom_call" | custom-call | flops 5000000 | bytes 2000000 | tf_op jit(solution)/shard_map/taper/pallas_call | solution.py:420
  59.2 9.1 %first.1 = (f32[320,128]{1,0:T(8,128)S(1)}, f32[320,128]{1,0:T(8,128)S(1)}, f32[320,128]{1,0:T(8,128)S(1)}, f32[320,128]{1,0:T(8,128)S(1)}, bf16[4,256,240]{2,1,...) custom-call(s32[5]{0:T(128)S(1)} %stack.24.place_ref, f32[4,256]{1,0:T(4,128)S(1)} %copy-done.4, ...), custom_call_target="tpu_custom_call" | custom-call | flops 3000000000 | bytes 8000000 | tf_op jit(solution)/shard_map/first/pallas_call | solution.py:435
  68.3 0.6 collective-permute-start.19
  68.8 2.6 %collective-permute-start.20 = (f32[320,128]{1,0:T(8,128)S(1)}, f32[320,128]{1,0:T(8,128)S(1)}, u32[]{:S(2)}, u32[]{:S(2)}) collective-permute-start(f32[320,128]{1,0:T(8,128)S(1)} %get-tuple-element.68), channel_id=1, source_target_pairs={{0,2},{1,3},{2,0},{3,1},{4,6},{5,7},{6,4},{7,5},{8,10},{9,11},{10,... | collective-permute-start | bytes 491528 | tf_op jit(solution)/shard_map/ppermute | solution.py:455
  71.4 0.4 collective-permute-start.21
  71.8 6.9 %second.1 = (f32[320,128]{1,0:T(8,128)S(1)}, f32[320,128]{1,0:T(8,128)S(1)}, f32[320,128]{1,0:T(8,128)S(1)}, f32[320,128]{1,0:T(8,128)S(1)}) custom-call(s32[5]{0:T(128)S(1)} %stack.24.place_ref, f32[160,512]{1,0:T(8,128)S(1)} %collective-permute-done.15.pack_ref, f32[8,80,512]{2,1,0:T(8,128)S(1)} %get-tuple-element.54.y_ref, ...), custom_call_target="tpu_custom_call" | custom-call | flops 3000000000 | bytes 8000000 | tf_op jit(solution)/shard_map/second/pallas_call | solution.py:456
  78.8 1.1 %collective-permute-start.16 = (f32[320,128]{1,0:T(8,128)S(1)}, f32[320,128]{1,0:T(8,128)S(1)}, u32[]{:S(2)}, u32[]{:S(2)}) collective-permute-start(f32[320,128]{1,0:T(8,128)S(1)} %get-tuple-element.63), channel_id=1, source_target_pairs={{0,1},{1,2},{2,3},{3,0},{4,5},{5,6},{6,7},{7,4},{8,9},{9,10},{10,1... | collective-permute-start | bytes 491528 | tf_op jit(solution)/shard_map/ppermute | solution.py:468
  79.9 0.6 collective-permute-start.17
  80.5 2.0 %collective-permute-start.18 = (f32[320,128]{1,0:T(8,128)S(1)}, f32[320,128]{1,0:T(8,128)S(1)}, u32[]{:S(2)}, u32[]{:S(2)}) collective-permute-start(f32[320,128]{1,0:T(8,128)S(1)} %get-tuple-element.65), channel_id=1, source_target_pairs={{0,3},{1,0},{2,1},{3,2},{4,7},{5,4},{6,5},{7,6},{8,11},{9,8},{10,9... | collective-permute-start | bytes 491528 | tf_op jit(solution)/shard_map/ppermute | solution.py:468
  82.5 1.5 %place.2.refs_3_ = f32[2560,128]{1,0:T(8,128)} custom-call(s32[5]{0:T(128)S(1)} %stack.24.place_ref, f32[320,128]{1,0:T(8,128)S(1)} %get-tuple-element.66.refs_0_, f32[320,128]{1,0:T(8,128)S(1)} %collective-permute-done.19.refs_1_, f32[320,128]{1,0:T(8,128)S(1)} %collective-permute-done.20.refs_2_, f32[320,128]{1,0:T(8,128)S(1)} %collective-permute-done.21.refs_3_, ...), custom_call_target="tpu_custom_call" | custom-call | tf_op jit(solution)/shard_map/place/pallas_call | solution.py:472
  84.0 1.8 %collective-permute-done.16.refs_0_ = f32[320,128]{1,0:T(8,128)S(1)} collective-permute-done((f32[320,128]{1,0:T(8,128)S(1)}, f32[320,128]{1,0:T(8,128)S(1)}, u32[]{:S(2)}, u32[]{:S(2)}) %collective-permute-start.16) | collective-permute-done | bytes 163872 | tf_op jit(solution)/shard_map/ppermute | solution.py:468
  85.8 1.8 %collective-permute-done.17.refs_1_ = f32[320,128]{1,0:T(8,128)S(1)} collective-permute-done((f32[320,128]{1,0:T(8,128)S(1)}, f32[320,128]{1,0:T(8,128)S(1)}, u32[]{:S(2)}, u32[]{:S(2)}) %collective-permute-start.17) | collective-permute-done | bytes 163872 | tf_op jit(solution)/shard_map/ppermute | solution.py:468
  87.6 1.4 %collective-permute-done.18.refs_2_ = f32[320,128]{1,0:T(8,128)S(1)} collective-permute-done((f32[320,128]{1,0:T(8,128)S(1)}, f32[320,128]{1,0:T(8,128)S(1)}, u32[]{:S(2)}, u32[]{:S(2)}) %collective-permute-start.18) | collective-permute-done | bytes 163872 | tf_op jit(solution)/shard_map/ppermute | solution.py:468
  89.0 1.3 %place.3 = f32[2560,128]{1,0:T(8,128)} custom-call(s32[5]{0:T(128)S(1)} %stack.24.place_ref, f32[320,128]{1,0:T(8,128)S(1)} %collective-permute-done.16.refs_0_, f32[320,128]{1,0:T(8,128)S(1)} %collective-permute-done.17.refs_1_, f32[320,128]{1,0:T(8,128)S(1)} %collective-permute-done.18.refs_2_, ...), custom_call_target="tpu_custom_call", output_to_operand_aliasing={{}: (4, {})} | custom-call | tf_op jit(solution)/shard_map/place/pallas_call | solution.py:472
  (24 shorter events, 0.1 us)
Async XLA Ops:
  0.1 1.3 %copy-start = (f32[16,20,8,128]{3,2,1,0:T(8,128)S(1)}, f32[16,20,8,128]{3,2,1,0:T(8,128)}, u32[]{:S(2)}) copy-start(f32[16,20,8,128]{3,2,1,0:T(8,128)} %param.6) | copy-start | bytes 3932164
  1.4 0.7 copy-start.1
  4.4 22.9 %collective-permute-start.5 = (f32[640,128]{1,0:T(8,128)S(1)}, f32[640,128]{1,0:T(8,128)S(1)}, u32[]{:S(2)}, u32[]{:S(2)}) collective-permute-start(f32[640,128]{1,0:T(8,128)S(1)} %get-tuple-element.41), channel_id=1, source_target_pairs={{0,3},{1,0},{2,1},{3,2},{4,7},{5,4},{6,5},{7,6},{8,11},{9,8},{10,9... | collective-permute-start | bytes 983048 | tf_op jit(solution)/shard_map/ppermute | solution.py:375
  8.1 19.2 %collective-permute-start.6 = (f32[640,128]{1,0:T(8,128)S(1)}, f32[640,128]{1,0:T(8,128)S(1)}, u32[]{:S(2)}, u32[]{:S(2)}) collective-permute-start(f32[640,128]{1,0:T(8,128)S(1)} %get-tuple-element.42), channel_id=1, source_target_pairs={{0,2},{1,3},{2,0},{3,1},{4,6},{5,7},{6,4},{7,5},{8,10},{9,11},{10,... | collective-permute-start | bytes 983048 | tf_op jit(solution)/shard_map/ppermute | solution.py:375
  8.4 18.9 %collective-permute-start.7 = (f32[640,128]{1,0:T(8,128)S(1)}, f32[640,128]{1,0:T(8,128)S(1)}, u32[]{:S(2)}, u32[]{:S(2)}) collective-permute-start(f32[640,128]{1,0:T(8,128)S(1)} %get-tuple-element.43), channel_id=1, source_target_pairs={{0,1},{1,2},{2,3},{3,0},{4,5},{5,6},{6,7},{7,4},{8,9},{9,10},{10,1... | collective-permute-start | bytes 983048 | tf_op jit(solution)/shard_map/ppermute | solution.py:375
  9.1 2.4 %collective-permute-start = (f32[20,512]{1,0:T(8,128)S(1)}, f32[20,512]{1,0:T(8,128)S(1)}, u32[]{:S(2)}, u32[]{:S(2)}) collective-permute-start(f32[20,512]{1,0:T(8,128)S(1)} %get-tuple-element.39), channel_id=1, source_target_pairs={{0,16},{16,0},{1,17},{17,1},{2,18},{18,2},{3,19},{19,3},{4,20},{20... | collective-permute-start | bytes 122888 | tf_op jit(solution)/shard_map/ppermute | solution.py:369
  11.5 8.5 %collective-permute-start.1 = (f32[20,512]{1,0:T(8,128)S(1)}, f32[20,512]{1,0:T(8,128)S(1)}, u32[]{:S(2)}, u32[]{:S(2)}) collective-permute-start(f32[20,512]{1,0:T(8,128)S(1)} %add.22), channel_id=1, source_target_pairs={{0,4},{4,0},{8,12},{12,8},{16,144},{20,148},{24,152},{28,156},{32,... | collective-permute-start | bytes 122888 | tf_op jit(solution)/shard_map/ppermute | solution.py:371
  20.0 35.8 %copy-start.2 = (s32[4,256]{1,0:T(4,128)S(1)}, s32[4,256]{1,0:T(4,128)}, u32[]{:S(2)}) copy-start(s32[4,256]{1,0:T(4,128)} %radius_ref.3) | copy-start | bytes 12292
  20.0 4.2 %collective-permute-start.2 = (f32[20,512]{1,0:T(8,128)S(1)}, f32[20,512]{1,0:T(8,128)S(1)}, u32[]{:S(2)}, u32[]{:S(2)}) collective-permute-start(f32[20,512]{1,0:T(8,128)S(1)} %add.23), channel_id=1, source_target_pairs={{0,8},{4,12},{8,0},{12,4},{16,80},{20,84},{24,88},{28,92},{32,40},... | collective-permute-start | bytes 122888 | tf_op jit(solution)/shard_map/ppermute | solution.py:371
  24.2 3.0 %collective-permute-start.3 = (f32[20,512]{1,0:T(8,128)S(1)}, f32[20,512]{1,0:T(8,128)S(1)}, u32[]{:S(2)}, u32[]{:S(2)}) collective-permute-start(f32[20,512]{1,0:T(8,128)S(1)} %add.24), channel_id=1, source_target_pairs={{0,32},{4,36},{8,40},{12,44},{16,48},{20,52},{24,56},{28,60},{32,0... | collective-permute-start | bytes 122888 | tf_op jit(solution)/shard_map/ppermute | solution.py:371
  28.8 17.7 %collective-permute-start.12 = (f32[80,512]{1,0:T(8,128)S(1)}, f32[80,512]{1,0:T(8,128)S(1)}, u32[]{:S(2)}, u32[]{:S(2)}) collective-permute-start(f32[80,512]{1,0:T(8,128)S(1)} %get-tuple-element.46), channel_id=1, source_target_pairs={{32,16},{64,48},{96,80},{128,112},{160,144},{192,176},{224,208},{1... | collective-permute-start | bytes 491528 | tf_op jit(solution)/shard_map/ppermute | solution.py:391
  31.6 3.0 %collective-permute-start.4 = (f32[20,512]{1,0:T(8,128)S(1)}, f32[20,512]{1,0:T(8,128)S(1)}, u32[]{:S(2)}, u32[]{:S(2)}) collective-permute-start(f32[20,512]{1,0:T(8,128)S(1)} %add.25.after_ref), channel_id=1, source_target_pairs={{0,64},{4,68},{8,72},{12,76},{16,20},{20,16},{24,28},{28,24},{32,9... | collective-permute-start | bytes 122888 | tf_op jit(solution)/shard_map/ppermute | solution.py:371
  34.6 6.3 %collective-permute-start.8 = (f32[20,512]{1,0:T(8,128)S(1)}, f32[20,512]{1,0:T(8,128)S(1)}, u32[]{:S(2)}, u32[]{:S(2)}) collective-permute-start(f32[20,512]{1,0:T(8,128)S(1)} %add.26), channel_id=1, source_target_pairs={{0,128},{4,132},{8,136},{12,140},{16,24},{20,28},{24,16},{28,20},{... | collective-permute-start | bytes 122888 | tf_op jit(solution)/shard_map/ppermute | solution.py:371
  37.5 6.1 %collective-permute-start.13 = (f32[80,128]{1,0:T(8,128)S(1)}, f32[80,128]{1,0:T(8,128)S(1)}, u32[]{:S(2)}, u32[]{:S(2)}) collective-permute-start(f32[80,128]{1,0:T(8,128)S(1)} %get-tuple-element.47), channel_id=1, source_target_pairs={{0,4},{4,8},{8,12},{1,5},{5,9},{9,13},{2,6},{6,10},{10,14},{3,7},{... | collective-permute-start | bytes 122888 | tf_op jit(solution)/shard_map/ppermute | solution.py:392
  39.7 5.0 %collective-permute-start.14 = (f32[80,128]{1,0:T(8,128)S(1)}, f32[80,128]{1,0:T(8,128)S(1)}, u32[]{:S(2)}, u32[]{:S(2)}) collective-permute-start(f32[80,128]{1,0:T(8,128)S(1)} %get-tuple-element.48), channel_id=1, source_target_pairs={{4,0},{8,4},{12,8},{5,1},{9,5},{13,9},{6,2},{10,6},{14,10},{7,3},{... | collective-permute-start | bytes 122888 | tf_op jit(solution)/shard_map/ppermute | solution.py:393
  41.0 4.2 %collective-permute-start.11 = (f32[20,512]{1,0:T(8,128)S(1)}, f32[20,512]{1,0:T(8,128)S(1)}, u32[]{:S(2)}, u32[]{:S(2)}) collective-permute-start(f32[20,512]{1,0:T(8,128)S(1)} %add.27.own_ref.after_ref), channel_id=1, source_target_pairs={{0,1},{1,2},{2,3},{3,0},{4,5},{5,6},{6,7},{7,4},{8,9},{9,10},{10,1... | collective-permute-start | bytes 122888 | tf_op jit(solution)/shard_map/ppermute | solution.py:399
  42.0 4.4 %collective-permute-start.10 = (f32[20,512]{1,0:T(8,128)S(1)}, f32[20,512]{1,0:T(8,128)S(1)}, u32[]{:S(2)}, u32[]{:S(2)}) collective-permute-start(f32[20,512]{1,0:T(8,128)S(1)} %add.27.own_ref.after_ref), channel_id=1, source_target_pairs={{0,2},{1,3},{2,0},{3,1},{4,6},{5,7},{6,4},{7,5},{8,10},{9,11},{10,... | collective-permute-start | bytes 122888 | tf_op jit(solution)/shard_map/ppermute | solution.py:399
  43.5 2.9 %collective-permute-start.9 = (f32[20,512]{1,0:T(8,128)S(1)}, f32[20,512]{1,0:T(8,128)S(1)}, u32[]{:S(2)}, u32[]{:S(2)}) collective-permute-start(f32[20,512]{1,0:T(8,128)S(1)} %add.27.own_ref.after_ref), channel_id=1, source_target_pairs={{0,3},{1,0},{2,1},{3,2},{4,7},{5,4},{6,5},{7,6},{8,11},{9,8},{10,9... | collective-permute-start | bytes 122888 | tf_op jit(solution)/shard_map/ppermute | solution.py:399
  46.5 12.7 %copy-start.3 = (f32[2,16,8,128]{3,2,1,0:T(8,128)S(1)}, f32[2,16,8,128]{3,2,1,0:T(8,128)}, u32[]{:S(2)}) copy-start(f32[2,16,8,128]{3,2,1,0:T(8,128)} %wind_ref.3) | copy-start | bytes 393220
  46.5 12.7 %copy-start.4 = (f32[4,256]{1,0:T(4,128)S(1)}, f32[4,256]{1,0:T(4,128)}, u32[]{:S(2)}) copy-start(f32[4,256]{1,0:T(4,128)} %value_ref.1) | copy-start | bytes 12292
  46.5 12.7 %copy-start.5 = (f32[4,256]{1,0:T(4,128)S(1)}, f32[4,256]{1,0:T(4,128)}, u32[]{:S(2)}) copy-start(f32[4,256]{1,0:T(4,128)} %error_ref.1) | copy-start | bytes 12292
  46.5 12.6 %collective-permute-start.15 = (f32[160,512]{1,0:T(8,128)S(1)}, f32[160,512]{1,0:T(8,128)S(1)}, u32[]{:S(2)}, u32[]{:S(2)}) collective-permute-start(f32[160,512]{1,0:T(8,128)S(1)} %stack.25.after_ref), channel_id=1, source_target_pairs={{0,16},{16,0},{1,17},{17,1},{2,18},{18,2},{3,19},{19,3},{4,20},{20... | collective-permute-start | bytes 983048 | tf_op jit(solution)/shard_map/ppermute | solution.py:418
  68.3 12.2 %collective-permute-start.19 = (f32[320,128]{1,0:T(8,128)S(1)}, f32[320,128]{1,0:T(8,128)S(1)}, u32[]{:S(2)}, u32[]{:S(2)}) collective-permute-start(f32[320,128]{1,0:T(8,128)S(1)} %get-tuple-element.67), channel_id=1, source_target_pairs={{0,1},{1,2},{2,3},{3,0},{4,5},{5,6},{6,7},{7,4},{8,9},{9,10},{10,1... | collective-permute-start | bytes 491528 | tf_op jit(solution)/shard_map/ppermute | solution.py:455
  68.8 13.6 %collective-permute-start.20 = (f32[320,128]{1,0:T(8,128)S(1)}, f32[320,128]{1,0:T(8,128)S(1)}, u32[]{:S(2)}, u32[]{:S(2)}) collective-permute-start(f32[320,128]{1,0:T(8,128)S(1)} %get-tuple-element.68), channel_id=1, source_target_pairs={{0,2},{1,3},{2,0},{3,1},{4,6},{5,7},{6,4},{7,5},{8,10},{9,11},{10,... | collective-permute-start | bytes 491528 | tf_op jit(solution)/shard_map/ppermute | solution.py:455
  71.4 11.1 %collective-permute-start.21 = (f32[320,128]{1,0:T(8,128)S(1)}, f32[320,128]{1,0:T(8,128)S(1)}, u32[]{:S(2)}, u32[]{:S(2)}) collective-permute-start(f32[320,128]{1,0:T(8,128)S(1)} %get-tuple-element.69), channel_id=1, source_target_pairs={{0,3},{1,0},{2,1},{3,2},{4,7},{5,4},{6,5},{7,6},{8,11},{9,8},{10,9... | collective-permute-start | bytes 491528 | tf_op jit(solution)/shard_map/ppermute | solution.py:455
  78.8 7.0 %collective-permute-start.16 = (f32[320,128]{1,0:T(8,128)S(1)}, f32[320,128]{1,0:T(8,128)S(1)}, u32[]{:S(2)}, u32[]{:S(2)}) collective-permute-start(f32[320,128]{1,0:T(8,128)S(1)} %get-tuple-element.63), channel_id=1, source_target_pairs={{0,1},{1,2},{2,3},{3,0},{4,5},{5,6},{6,7},{7,4},{8,9},{9,10},{10,1... | collective-permute-start | bytes 491528 | tf_op jit(solution)/shard_map/ppermute | solution.py:468
  79.9 7.8 %collective-permute-start.17 = (f32[320,128]{1,0:T(8,128)S(1)}, f32[320,128]{1,0:T(8,128)S(1)}, u32[]{:S(2)}, u32[]{:S(2)}) collective-permute-start(f32[320,128]{1,0:T(8,128)S(1)} %get-tuple-element.64), channel_id=1, source_target_pairs={{0,2},{1,3},{2,0},{3,1},{4,6},{5,7},{6,4},{7,5},{8,10},{9,11},{10,... | collective-permute-start | bytes 491528 | tf_op jit(solution)/shard_map/ppermute | solution.py:468
  80.5 8.5 %collective-permute-start.18 = (f32[320,128]{1,0:T(8,128)S(1)}, f32[320,128]{1,0:T(8,128)S(1)}, u32[]{:S(2)}, u32[]{:S(2)}) collective-permute-start(f32[320,128]{1,0:T(8,128)S(1)} %get-tuple-element.65), channel_id=1, source_target_pairs={{0,3},{1,0},{2,1},{3,2},{4,7},{5,4},{6,5},{7,6},{8,11},{9,8},{10,9... | collective-permute-start | bytes 491528 | tf_op jit(solution)/shard_map/ppermute | solution.py:468
